TPU v7x, 32 devices: a whole 2x2x4 slice. The times are simulated.
32 devices in a mesh: region: 4 (over x, core), sector: 8 (over z, y).
Axes of the slice: x: 2, y: 2, z: 4, core: 2. Of those that a mesh axis runs over, the one named last changes fastest.
Arguments:
- start_state: bfloat16 [4, 32, 128, 4, 128], P('region', 'sector'), may hold values from -6 to 6
- left_env: bfloat16 [4, 32, 16, 128, 128], P('region', 'sector'), may hold values from -0.125 to 0.125
- right_env: bfloat16 [4, 32, 16, 128, 128], P('region', 'sector'), may hold values from -0.5 to 0.5
- mpo_tensor: bfloat16 [16, 4, 4, 16], replicated, may hold values from -0.75 to 0.75
- decay: float32 [4, 32, 128], P('region', 'sector'), may hold values from 0.15 to 1
- energy_terms: float32 [4, 32, 128], P('region', 'sector'), may hold values from -1.2 to 1.2
- live_count: int32 [4, 8], P('region', 'sector'), may hold values from 1 to 4, as said below
Outputs:
- state_out: bfloat16 [4, 32, 128, 4, 128], P('region', 'sector')
- density: float32 [4, 32, 128, 128], P('region', 'sector')
- energy: float32 [4], P('region')
Inputs may be any that keep to these rules, and one draw needn't show every extreme that they name: `live_count`: each device's live blocks fill its first slots; some device holds 4 live blocks.
All inputs are finite; a program needn't handle non-finite values.
Results may differ from a plain program's by a relative error of at most 0.0055.
The roundings to bfloat16 on the way count: a program that leaves them out, or rounds other values in their place, can miss the bound.
Values may be sent and summed in bfloat16 or wider, within the bound.
A program may use at most 64 MiB of HBM per device.

v0:
```python
import functools
import math

import jax
import jax.numpy as jnp
from jax import lax
from jax.experimental import pallas as pl
from jax.experimental.pallas import tpu as pltpu
from jax.sharding import PartitionSpec as P

DAV = 2
EPS = 1e-06
MESH = pl.DeviceIdType.MESH
F32 = jnp.float32
BF16 = jnp.bfloat16
PAD = 8


def half_rotation(y, x):
    top = jnp.maximum(jnp.abs(x), jnp.abs(y))
    safe = jnp.where(top > 0, top, 1.0)
    xn, yn = x / safe, y / safe
    h = jnp.sqrt(xn * xn + yn * yn)
    h = jnp.where(top > 0, h, 1.0)
    big = jnp.sqrt(0.5 * (h + jnp.abs(xn)) / h)
    small = jnp.abs(yn) / (2.0 * h * big)
    big = jnp.where(top > 0, big, 1.0)
    small = jnp.where(top > 0, small, 0.0)
    cos_part = jnp.where(x >= 0, big, small)
    sin_size = jnp.where(x >= 0, small, big)
    return cos_part, jnp.where(y > 0, sin_size, -sin_size)


def kernel(
    regions, sectors, start, left, right, operator, decay, energy, live,
    state_out, energy_out,
    start_in, left_in, left_t, right_in, right_t, planes, rows_buf, mixed, lines, spread,
    current, applied, search, image, decay_all, energy_all, shift, part, gathered,
    left_send, left_recv, right_sem, own_sem, start_sem, pre_send, pre_recv, sum_send, sum_recv,
):
    slots, chan, blk, _ = left.shape
    phys = start.shape[1] // blk
    wide = phys * blk
    me, mine = lax.axis_index("region"), lax.axis_index("sector")
    group = 256 // (phys * chan)
    pair = 2 * group
    for n in range(slots):
        pltpu.make_async_copy(right.at[n], right_in.at[n], right_sem.at[n]).start()
        pltpu.make_async_copy(start.at[n], start_in.at[n], start_sem.at[n]).start()

    barrier = pltpu.get_barrier_semaphore()
    for k in range(1, regions):
        pl.semaphore_signal(
            barrier, 1, device_id={"region": lax.rem(me + k, regions)}, device_id_type=MESH
        )
    for k in range(1, sectors):
        pl.semaphore_signal(
            barrier, 1, device_id={"sector": lax.rem(mine + k, sectors)}, device_id_type=MESH
        )
    pl.semaphore_wait(barrier, regions + sectors - 2)

    def left_copy(n):
        return pltpu.make_async_remote_copy(
            src_ref=left.at[n], dst_ref=left_in.at[n],
            send_sem=left_send.at[n], recv_sem=left_recv.at[n],
            device_id={"region": lax.rem(me + 1, regions)}, device_id_type=MESH,
        )

    def own_copy(n):
        return pltpu.make_async_copy(left.at[n], left_in.at[n], own_sem.at[n])

    def prefix_copies(k, slot):
        to = {"region": lax.rem(me + k, regions)}
        return [
            pltpu.make_async_remote_copy(
                src_ref=src, dst_ref=dst.at[slot],
                send_sem=pre_send.at[i, k - 1], recv_sem=pre_recv.at[i, k - 1],
                device_id=to, device_id_type=MESH,
            )
            for i, (src, dst) in enumerate(((decay, decay_all), (energy, energy_all)))
        ]

    for k in range(1, regions):
        for copy in prefix_copies(k, me):
            copy.start()

    @pl.when(me < regions - 1)
    def _():
        for n in range(slots):
            left_copy(n).start()

    @pl.when(me == 0)
    def _():
        for n in range(slots):
            own_copy(n).start()

    decay_all[me] = decay[...]
    energy_all[me] = energy[...]
    for k in range(1, regions):
        for copy in prefix_copies(k, lax.rem(me + regions - k, regions)):
            copy.wait()
    offsets = jnp.zeros((slots, blk), F32)
    for p in range(regions - 1):
        offsets = jnp.where(p < me, decay_all[p] * offsets + energy_all[p], offsets)
    shift[...] = offsets

    live_slots = live[...]

    side = group * phys * chan
    lines[...] = operator[...].astype(F32)

    def where_one(test):
        return jnp.where(test, 1.0, 0.0).astype(BF16)

    def grid_of(shape):
        return [lax.broadcasted_iota(jnp.int32, shape, i) for i in range(2)]

    r, c = grid_of((side, chan * phys))
    pick_row = where_one((r // (group * phys) == c // phys) & (r % phys == c % phys))
    r, c = grid_of((chan, side))
    total = jnp.zeros((side, side), F32)
    for t in range(phys):
        tall = jnp.dot(
            pick_row,
            lines[pl.ds(t, chan * phys, stride=phys), :].astype(BF16),
            preferred_element_type=F32,
        ).astype(BF16)
        pick_column = where_one((c // (group * chan) == t) & (c % chan == r))
        total = total + jnp.dot(tall, pick_column, preferred_element_type=F32)
    r, c = grid_of((side, side))
    same = (r // phys) % group == (c // chan) % group
    spread[...] = jnp.where(same, total, 0.0).astype(BF16)

    def prepare_right(n):
        pltpu.make_async_copy(right.at[n], right_in.at[n], right_sem.at[n]).wait()
        pitch = blk + PAD
        for w in range(chan):
            planes[w * pitch : w * pitch + blk, :] = right_in[n, w].astype(F32).T
        for b in range(blk):
            right_t[n, b * chan : (b + 1) * chan, :] = planes[
                pl.ds(b, chan, stride=pitch), :
            ].astype(BF16)

    def prepare_left(n):
        for u in range(chan):
            left_t[n, u * blk : (u + 1) * blk, :] = left_in[n, u].T

    def sum8(value):
        return jnp.sum(value.reshape(-1, 8, value.shape[-1]), axis=0)

    def operate(n, slot, vector, arrive):
        half = group * chan
        for j in range(blk // pair):
            rows = right_t[n, j * pair * chan : (j + 1) * pair * chan, :]
            first = jnp.dot(rows, vector, preferred_element_type=F32).astype(BF16)
            stacked = [
                jnp.concatenate(
                    [
                        first[g * half : (g + 1) * half, t * blk : (t + 1) * blk]
                        for t in range(phys)
                    ],
                    axis=0,
                )
                for g in range(2)
            ]
            second = jnp.dot(
                spread[...], jnp.concatenate(stacked, axis=1), preferred_element_type=F32
            ).astype(BF16)
            tile = group * phys
            for g in range(2):
                row = (2 * j + g) * tile
                for u in range(chan):
                    mixed[slot, row : row + tile, u * blk : (u + 1) * blk] = second[
                        u * tile : (u + 1) * tile, g * blk : (g + 1) * blk
                    ]
        arrive()
        rows_buf[slot] = jnp.dot(mixed[slot], left_t[n], preferred_element_type=F32)
        return [rows_buf[slot, pl.ds(s, blk, stride=phys), :] for s in range(phys)]

    def reduce(turn, sums):
        line = lax.broadcasted_iota(jnp.int32, (8, blk), 0)
        tile = jnp.zeros((8, blk), F32)
        for q, total in enumerate(sums):
            tile = jnp.where(line == q, jnp.sum(total, axis=0, keepdims=True), tile)
        part[turn] = tile
        gathered[turn, mine] = tile

        def copy_of(k, slot):
            return pltpu.make_async_remote_copy(
                src_ref=part.at[turn], dst_ref=gathered.at[turn, slot],
                send_sem=sum_send.at[turn, k - 1], recv_sem=sum_recv.at[turn, k - 1],
                device_id={"sector": lax.rem(mine + k, sectors)}, device_id_type=MESH,
            )

        for k in range(1, sectors):
            copy_of(k, mine).start()
        for k in range(1, sectors):
            copy_of(k, lax.rem(mine + sectors - k, sectors)).wait()
        total = gathered[turn, 0]
        for i in range(1, sectors):
            total = total + gathered[turn, i]
        total = jnp.broadcast_to(jnp.sum(total, axis=1, keepdims=True), (8, blk))
        return [total[q : q + 1] for q in range(len(sums))]

    zero = jnp.zeros((8, blk), F32)

    def open_slot(n, sums):
        prepare_right(n)
        alive = jnp.broadcast_to(jnp.where(n < live_slots, 1.0, 0.0), (1, blk)).astype(F32)
        pltpu.make_async_copy(start.at[n], start_in.at[n], start_sem.at[n]).wait()
        rows_buf[0] = start_in[n].astype(F32)
        firsts = []
        for t in range(phys):
            first = rows_buf[0, pl.ds(t, blk, stride=phys), :].T * alive
            current[n, t] = first
            firsts.append(first.astype(BF16))
        offset = shift[pl.ds(n, 1)]

        def arrive():
            @pl.when(me > 0)
            def _():
                left_copy(n).wait_recv()

            @pl.when(me == 0)
            def _():
                own_copy(n).wait()

            prepare_left(n)

        results = operate(n, 0, jnp.concatenate(firsts, axis=1), arrive)
        a, b, c = sums
        for s in range(phys):
            first = current[n, s]
            value = results[s] + offset * first
            applied[n, s] = value
            a, b, c = a + sum8(first * first), b + sum8(first * value), c + sum8(value * value)
        return a, b, c

    sums = lax.fori_loop(0, slots, open_slot, (zero, zero, zero))
    norm_sum, first_quotient, first_sq = reduce(0, sums)
    inverse = lax.rsqrt(norm_sum + EPS)
    quotient = first_quotient * inverse * inverse
    image_sq = first_sq * inverse * inverse
    weight = norm_sum / (norm_sum + EPS)
    cos_part = inverse
    sin_part = None
    for turn in range(DAV):
        resid_sq = image_sq - quotient * quotient * (2.0 - weight)
        factor = lax.rsqrt(resid_sq + EPS)

        def next_slot(n, sums, cos_part=cos_part, sin_part=sin_part, quotient=quotient, factor=factor):
            probes = []
            for t in range(phys):
                state, moved = cos_part * current[n, t], cos_part * applied[n, t]
                if sin_part is not None:
                    state = state + sin_part * search[n, t]
                    moved = moved + sin_part * image[n, t]
                current[n, t] = state
                applied[n, t] = moved
                probe = (moved - quotient * state) * factor
                search[n, t] = probe
                probes.append(probe.astype(BF16))
            results = operate(n, 0, jnp.concatenate(probes, axis=1), lambda: None)
            offset = shift[pl.ds(n, 1)]
            a, b, c = sums
            for s in range(phys):
                value = results[s] + offset * search[n, s].astype(BF16).astype(F32)
                image[n, s] = value
                a = a + sum8(current[n, s] * value)
                b = b + sum8(applied[n, s] * value)
                c = c + sum8(value * value)
            return a, b, c

        sums = lax.fori_loop(0, slots, next_slot, (zero, zero, zero))
        along_state, along_image, search_sq = reduce(turn + 1, sums)
        curvature = factor * (along_image - quotient * along_state)
        cos_part, sin_part = half_rotation(-2.0 * resid_sq * factor, curvature - quotient)
        cross_term = factor * (image_sq - quotient * quotient)
        inner_term = factor * quotient * (1.0 - weight)
        next_quotient = (
            cos_part * cos_part * quotient
            + cos_part * sin_part * (along_state + cross_term)
            + sin_part * sin_part * curvature
        )
        next_sq = (
            cos_part * cos_part * image_sq
            + 2.0 * cos_part * sin_part * along_image
            + sin_part * sin_part * search_sq
        )
        weight = (
            cos_part * cos_part * weight
            + 2.0 * cos_part * sin_part * inner_term
            + sin_part * sin_part * resid_sq * factor * factor
        )
        quotient, image_sq = next_quotient, next_sq

    energy_out[...] = jnp.broadcast_to(quotient, (8, blk))
    scale = math.sqrt(slots * sectors * blk * phys * blk)

    for n in range(slots):
        for t in range(phys):
            state = cos_part * current[n, t] + sin_part * search[n, t]
            state_out[n, t] = (scale * state).astype(BF16)

    @pl.when(me < regions - 1)
    def _():
        for n in range(slots):
            left_copy(n).wait_send()


def finish(state, energy, out, density, energy_out, rows_buf, out_buf, density_buf, sems):
    slots, phys, blk, _ = state.shape
    copies = []
    for n in range(slots):
        total = jnp.zeros((blk, blk), F32)
        for s in range(phys):
            turned = state[n, s].T
            rows_buf[n, pl.ds(s, blk, stride=phys), :] = turned.astype(F32)
            total = total + jnp.dot(turned, state[n, s], preferred_element_type=F32)
        out_buf[n] = rows_buf[n].astype(BF16)
        density_buf[n] = total / (phys * blk)
        for i, (src, dst) in enumerate(((out_buf, out), (density_buf, density))):
            copies.append(pltpu.make_async_copy(src.at[n], dst.at[n], sems.at[i, n]))
            copies[-1].start()
    energy_out[0] = energy[0, 0]
    for copy in copies:
        copy.wait()


def body(regions, sectors, start_state, left_env, right_env, mpo_tensor, decay, energy_terms, live_count):
    _, slots, blk, phys, _ = start_state.shape
    chan = left_env.shape[2]
    wide = phys * blk
    group = 256 // (phys * chan)
    vmem = pl.BlockSpec(memory_space=pltpu.VMEM)
    hbm = pl.BlockSpec(memory_space=pl.ANY)
    smem = pl.BlockSpec(memory_space=pltpu.SMEM)
    dma = pltpu.SemaphoreType.DMA
    state = pltpu.VMEM((slots, phys, blk, blk), F32)
    outs = pl.pallas_call(
        functools.partial(kernel, regions, sectors),
        out_shape=(
            jax.ShapeDtypeStruct((slots, phys, blk, blk), BF16),
            jax.ShapeDtypeStruct((8, blk), F32),
        ),
        in_specs=[hbm, hbm, hbm, vmem, vmem, vmem, vmem],
        out_specs=(vmem, vmem),
        scratch_shapes=[
            pltpu.VMEM((slots, wide, blk), BF16),
            pltpu.VMEM((slots, chan, blk, blk), BF16),
            pltpu.VMEM((slots, chan * blk, blk), BF16),
            pltpu.VMEM((slots, chan, blk, blk), BF16),
            pltpu.VMEM((slots, chan * blk, blk), BF16),
            pltpu.VMEM((chan * (blk + PAD), blk), F32),
            pltpu.VMEM((2, wide, blk), F32),
            pltpu.VMEM((2, wide, chan * blk), BF16),
            pltpu.VMEM((chan * phys * phys, chan), F32),
            pltpu.VMEM((group * phys * chan, group * phys * chan), BF16),
            state, state, state, state,
            pltpu.VMEM((regions, slots, blk), F32),
            pltpu.VMEM((regions, slots, blk), F32),
            pltpu.VMEM((slots, blk), F32),
            pltpu.VMEM((DAV + 1, 8, blk), F32),
            pltpu.VMEM((DAV + 1, sectors, 8, blk), F32),
            dma((slots,)), dma((slots,)), dma((slots,)), dma((slots,)), dma((slots,)),
            dma((2, regions)), dma((2, regions)),
            dma((DAV + 1, sectors)), dma((DAV + 1, sectors)),
        ],
        compiler_params=pltpu.CompilerParams(collective_id=0, has_side_effects=True),
    )(
        start_state.reshape(slots, wide, blk), left_env[0], right_env[0],
        mpo_tensor.reshape(chan * phys * phys, chan),
        decay[0], energy_terms[0], live_count,
    )
    state_out, density, energy = pl.pallas_call(
        finish,
        out_shape=(
            jax.ShapeDtypeStruct((slots, wide, blk), BF16),
            jax.ShapeDtypeStruct((slots, blk, blk), F32),
            jax.ShapeDtypeStruct((1,), F32),
        ),
        in_specs=[vmem, vmem],
        out_specs=(hbm, hbm, smem),
        scratch_shapes=[
            pltpu.VMEM((slots, wide, blk), F32),
            pltpu.VMEM((slots, wide, blk), BF16),
            pltpu.VMEM((slots, blk, blk), F32),
            dma((2, slots)),
        ],
    )(*outs)
    return (
        state_out.reshape(start_state.shape),
        density.reshape(1, slots, blk, blk),
        energy,
    )


def solution(mesh):
    in_specs = (
        P("region", "sector", None, None, None),
        P("region", "sector", None, None, None),
        P("region", "sector", None, None, None),
        P(),
        P("region", "sector", None),
        P("region", "sector", None),
        P("region", "sector"),
    )
    out_specs = (
        P("region", "sector", None, None, None),
        P("region", "sector", None, None),
        P("region"),
    )
    step = functools.partial(body, mesh.shape["region"], mesh.shape["sector"])
    return jax.shard_map(step, mesh=mesh, in_specs=in_specs, out_specs=out_specs, check_vma=False)
```

profile of v0, /device:TPU:2, one launch (start us, length us, event | category | flops | bytes accessed | tf_op | source)
XLA Modules:
  0.0 65.4 jit_solution(589796659616348689)
XLA Ops:
  1.3 61.3 %shard_map.94 = (bf16[4,4,128,128]{3,2,1,0:T(8,128)(2,1)}, f32[8,128]{1,0:T(8,128)}) custom-call(bf16[4,512,128]{2,1,0:T(8,128)(2,1)} %bitcast.10, bf16[4,16,128,128]{3,2,1,0:T(8,128)(2,1)} %bitcast.8, bf16[4,16,128,128]{3,2,1,0:T(8,128)(2,1)} %bitcast.9, bf16[256,16]{1,0:T(8,128)(2,1)} %bitcast.11, f32[4,128]{1,0:T(4,128)} %bitcast.12, f32[4,128]{1,0:T(4,128)} %bitcast.13, ...), custom_call_target="tpu_custom_call" | custom-call | tf_op jit(solution)/shard_map/pallas_call | solution.py:340
  62.6 2.7 %shard_map.95 = (bf16[4,512,128]{2,1,0:T(8,128)(2,1)}, f32[4,128,128]{2,1,0:T(8,128)}, f32[1]{0:T(128)}) custom-call(bf16[4,4,128,128]{3,2,1,0:T(8,128)(2,1)} %get-tuple-element.8.state, f32[8,128]{1,0:T(8,128)} %get-tuple-element.9.energy), custom_call_target="tpu_custom_call" | custom-call | tf_op jit(solution)/shard_map/pallas_call | solution.py:375
where the time goes:
time: 65.5 us; the launch traced here: 65.4 us
  Pallas kernels  64.1 us (98%)
  between operations  1.29 us (2%)
    pallas_call x1, Pallas kernels, body(): pl.pallas_call(functools.partial(kernel, regions, sectors), out_shape=(ja...  61.3 us
    pallas_call x1, Pallas kernels, body(): pl.pallas_call(finish, out_shape=(jax.ShapeDtypeStruct((slots, wide, blk)...  2.73 us

commit v1 on v0

--- a/solution.py
+++ b/solution.py
@@ -35,7 +35,7 @@
     regions, sectors, start, left, right, operator, decay, energy, live,
     state_out, energy_out,
     start_in, left_in, left_t, right_in, right_t, planes, rows_buf, mixed, lines, spread,
-    current, applied, search, image, decay_all, energy_all, shift, part, gathered,
+    base0, base1, base2, image, decay_all, energy_all, shift, part, gathered,
     left_send, left_recv, right_sem, own_sem, start_sem, pre_send, pre_recv, sum_send, sum_recv,
 ):
     slots, chan, blk, _ = left.shape
@@ -177,34 +177,21 @@
         rows_buf[slot] = jnp.dot(mixed[slot], left_t[n], preferred_element_type=F32)
         return [rows_buf[slot, pl.ds(s, blk, stride=phys), :] for s in range(phys)]
 
-    def reduce(turn, sums):
-        line = lax.broadcasted_iota(jnp.int32, (8, blk), 0)
-        tile = jnp.zeros((8, blk), F32)
-        for q, total in enumerate(sums):
-            tile = jnp.where(line == q, jnp.sum(total, axis=0, keepdims=True), tile)
-        part[turn] = tile
-        gathered[turn, mine] = tile
-
-        def copy_of(k, slot):
-            return pltpu.make_async_remote_copy(
-                src_ref=part.at[turn], dst_ref=gathered.at[turn, slot],
-                send_sem=sum_send.at[turn, k - 1], recv_sem=sum_recv.at[turn, k - 1],
-                device_id={"sector": lax.rem(mine + k, sectors)}, device_id_type=MESH,
-            )
-
-        for k in range(1, sectors):
-            copy_of(k, mine).start()
-        for k in range(1, sectors):
-            copy_of(k, lax.rem(mine + sectors - k, sectors)).wait()
-        total = gathered[turn, 0]
-        for i in range(1, sectors):
-            total = total + gathered[turn, i]
-        total = jnp.broadcast_to(jnp.sum(total, axis=1, keepdims=True), (8, blk))
-        return [total[q : q + 1] for q in range(len(sums))]
+    def spread_sum(total):
+        return jnp.broadcast_to(jnp.sum(total, keepdims=True).reshape(1, 1), (1, blk))
+
+    def length_of(square, whole):
+        square = jnp.maximum(square, 1e-10 * whole)
+        inverse = jnp.where(square > 0, lax.rsqrt(jnp.where(square > 0, square, 1.0)), 0.0)
+        return square * inverse, inverse
+
+    def share_of(value, norm):
+        return jnp.where(norm > 0, value / jnp.where(norm > 0, norm, 1.0), 0.0)
 
     zero = jnp.zeros((8, blk), F32)
-
-    def open_slot(n, sums):
+    lane = lax.broadcasted_iota(jnp.int32, (1, blk), 1)
+
+    def solve_slot(n, carry):
         prepare_right(n)
         alive = jnp.broadcast_to(jnp.where(n < live_slots, 1.0, 0.0), (1, blk)).astype(F32)
         pltpu.make_async_copy(start.at[n], start_in.at[n], start_sem.at[n]).wait()
@@ -212,7 +199,7 @@
         firsts = []
         for t in range(phys):
             first = rows_buf[0, pl.ds(t, blk, stride=phys), :].T * alive
-            current[n, t] = first
+            base0[n, t] = first
             firsts.append(first.astype(BF16))
         offset = shift[pl.ds(n, 1)]
 
@@ -228,79 +215,129 @@
             prepare_left(n)
 
         results = operate(n, 0, jnp.concatenate(firsts, axis=1), arrive)
-        a, b, c = sums
+        ff, fa, aa = zero, zero, zero
         for s in range(phys):
-            first = current[n, s]
+            first = base0[n, s]
             value = results[s] + offset * first
-            applied[n, s] = value
-            a, b, c = a + sum8(first * first), b + sum8(first * value), c + sum8(value * value)
-        return a, b, c
-
-    sums = lax.fori_loop(0, slots, open_slot, (zero, zero, zero))
-    norm_sum, first_quotient, first_sq = reduce(0, sums)
-    inverse = lax.rsqrt(norm_sum + EPS)
-    quotient = first_quotient * inverse * inverse
-    image_sq = first_sq * inverse * inverse
-    weight = norm_sum / (norm_sum + EPS)
-    cos_part = inverse
-    sin_part = None
+            image[s] = value
+            ff, fa, aa = ff + sum8(first * first), fa + sum8(first * value), aa + sum8(value * value)
+        ff, fa, aa = spread_sum(ff), spread_sum(fa), spread_sum(aa)
+        sigma = share_of(fa, ff)
+        rho1, inverse = length_of(aa - sigma * fa, aa)
+
+        probes = []
+        g01, g11 = zero, zero
+        for t in range(phys):
+            first = base0[n, t]
+            probe = (image[t] - sigma * first) * inverse
+            base1[n, t] = probe
+            g01, g11 = g01 + sum8(first * probe), g11 + sum8(probe * probe)
+            probes.append(probe.astype(BF16))
+        results = operate(n, 0, jnp.concatenate(probes, axis=1), lambda: None)
+        fa, pa, aa = zero, zero, zero
+        for s in range(phys):
+            probe = base1[n, s]
+            value = results[s] + offset * probe.astype(BF16).astype(F32)
+            image[s] = value
+            fa, pa, aa = fa + sum8(base0[n, s] * value), pa + sum8(probe * value), aa + sum8(value * value)
+        g01, g11, fa, pa, aa = spread_sum(g01), spread_sum(g11), spread_sum(fa), spread_sum(pa), spread_sum(aa)
+        alpha, beta = share_of(fa, ff), share_of(pa, g11)
+        rho2, inverse = length_of(aa - alpha * fa - beta * pa, aa)
+
+        probes = []
+        g02, g12, g22 = zero, zero, zero
+        for t in range(phys):
+            probe = (image[t] - alpha * base0[n, t] - beta * base1[n, t]) * inverse
+            base2[n, t] = probe
+            g02, g12, g22 = g02 + sum8(base0[n, t] * probe), g12 + sum8(base1[n, t] * probe), g22 + sum8(probe * probe)
+            probes.append(probe.astype(BF16))
+        results = operate(n, 0, jnp.concatenate(probes, axis=1), lambda: None)
+        g03, g13, g23 = zero, zero, zero
+        for s in range(phys):
+            probe = base2[n, s]
+            value = results[s] + offset * probe.astype(BF16).astype(F32)
+            g03, g13, g23 = g03 + sum8(base0[n, s] * value), g13 + sum8(base1[n, s] * value), g23 + sum8(probe * value)
+        numbers = [ff, sigma, rho1, g01, g11, alpha, beta, rho2]
+        numbers += [spread_sum(g) for g in (g02, g12, g22, g03, g13, g23)]
+        here = lane == mine * slots + n
+        for i, number in enumerate(numbers):
+            part[i : i + 1] = jnp.where(here, number, part[i : i + 1])
+        return carry
+
+    part[...] = jnp.zeros_like(part)
+    lax.fori_loop(0, slots, solve_slot, 0)
+
+    gathered[mine] = part[...]
+
+    def copy_of(k, slot):
+        return pltpu.make_async_remote_copy(
+            src_ref=part, dst_ref=gathered.at[slot],
+            send_sem=sum_send.at[k - 1], recv_sem=sum_recv.at[k - 1],
+            device_id={"sector": lax.rem(mine + k, sectors)}, device_id_type=MESH,
+        )
+
+    for k in range(1, sectors):
+        copy_of(k, mine).start()
+    for k in range(1, sectors):
+        copy_of(k, lax.rem(mine + sectors - k, sectors)).wait()
+    table = gathered[0]
+    for i in range(1, sectors):
+        table = table + gathered[i]
+    (
+        g00, sigma, rho1, g01, g11, alpha, beta, rho2, g02, g12, g22, g03, g13, g23,
+    ) = [table[i : i + 1] for i in range(14)]
+    gram = {
+        (0, 0): g00, (0, 1): g01, (0, 2): g02, (0, 3): g03, (1, 1): g11, (1, 2): g12, (1, 3): g13,
+        (2, 2): g22, (2, 3): g23,
+    }
+
+    def inner(x, y):
+        total = jnp.zeros((1, blk), F32)
+        for i, xi in enumerate(x):
+            for j, yj in enumerate(y):
+                if xi is not None and yj is not None:
+                    total = total + xi * yj * gram[min(i, j), max(i, j)]
+        return jnp.broadcast_to(jnp.sum(total, axis=1, keepdims=True), (1, blk))
+
+    def mix(p, x, q, y):
+        def one(a, b):
+            if a is None:
+                return None if b is None else q * b
+            return p * a if b is None else p * a + q * b
+
+        return [one(a, b) for a, b in zip(x, y)]
+
+    images = [[sigma, rho1, None, None], [alpha, beta, rho2, None], [None, None, None, jnp.ones((1, blk), F32)]]
+    unit = jnp.ones((1, blk), F32)
+    inverse = lax.rsqrt(inner([unit], [unit]) + EPS)
+    current = [inverse * unit, None, None, None]
+    applied = [inverse * a if a is not None else None for a in images[0]]
     for turn in range(DAV):
-        resid_sq = image_sq - quotient * quotient * (2.0 - weight)
+        quotient = inner(current, applied)
+        residual = mix(1.0, applied, -quotient, current)
+        resid_sq = inner(residual, residual)
         factor = lax.rsqrt(resid_sq + EPS)
-
-        def next_slot(n, sums, cos_part=cos_part, sin_part=sin_part, quotient=quotient, factor=factor):
-            probes = []
-            for t in range(phys):
-                state, moved = cos_part * current[n, t], cos_part * applied[n, t]
-                if sin_part is not None:
-                    state = state + sin_part * search[n, t]
-                    moved = moved + sin_part * image[n, t]
-                current[n, t] = state
-                applied[n, t] = moved
-                probe = (moved - quotient * state) * factor
-                search[n, t] = probe
-                probes.append(probe.astype(BF16))
-            results = operate(n, 0, jnp.concatenate(probes, axis=1), lambda: None)
-            offset = shift[pl.ds(n, 1)]
-            a, b, c = sums
-            for s in range(phys):
-                value = results[s] + offset * search[n, s].astype(BF16).astype(F32)
-                image[n, s] = value
-                a = a + sum8(current[n, s] * value)
-                b = b + sum8(applied[n, s] * value)
-                c = c + sum8(value * value)
-            return a, b, c
-
-        sums = lax.fori_loop(0, slots, next_slot, (zero, zero, zero))
-        along_state, along_image, search_sq = reduce(turn + 1, sums)
-        curvature = factor * (along_image - quotient * along_state)
+        search = [factor * a if a is not None else None for a in residual]
+        moved = [None] * 4
+        for a, line in zip(search, images):
+            if a is not None:
+                moved = mix(1.0, moved, a, line)
+        curvature = inner(search, moved)
         cos_part, sin_part = half_rotation(-2.0 * resid_sq * factor, curvature - quotient)
-        cross_term = factor * (image_sq - quotient * quotient)
-        inner_term = factor * quotient * (1.0 - weight)
-        next_quotient = (
-            cos_part * cos_part * quotient
-            + cos_part * sin_part * (along_state + cross_term)
-            + sin_part * sin_part * curvature
-        )
-        next_sq = (
-            cos_part * cos_part * image_sq
-            + 2.0 * cos_part * sin_part * along_image
-            + sin_part * sin_part * search_sq
-        )
-        weight = (
-            cos_part * cos_part * weight
-            + 2.0 * cos_part * sin_part * inner_term
-            + sin_part * sin_part * resid_sq * factor * factor
-        )
-        quotient, image_sq = next_quotient, next_sq
-
-    energy_out[...] = jnp.broadcast_to(quotient, (8, blk))
+        current = mix(cos_part, current, sin_part, search)
+        applied = mix(cos_part, applied, sin_part, moved)
+    energy_out[...] = jnp.broadcast_to(inner(current, applied), (8, blk))
     scale = math.sqrt(slots * sectors * blk * phys * blk)
 
     for n in range(slots):
+        here = lane == mine * slots + n
+        c0, c1, c2 = [
+            jnp.broadcast_to(jnp.sum(jnp.where(here, scale * c, 0.0), axis=1, keepdims=True), (1, blk))
+            for c in current[:3]
+        ]
         for t in range(phys):
-            state = cos_part * current[n, t] + sin_part * search[n, t]
-            state_out[n, t] = (scale * state).astype(BF16)
+            state = c0 * base0[n, t] + c1 * base1[n, t] + c2 * base2[n, t]
+            state_out[n, t] = state.astype(BF16)
 
     @pl.when(me < regions - 1)
     def _():
@@ -356,15 +393,15 @@
             pltpu.VMEM((2, wide, chan * blk), BF16),
             pltpu.VMEM((chan * phys * phys, chan), F32),
             pltpu.VMEM((group * phys * chan, group * phys * chan), BF16),
-            state, state, state, state,
+            state, state, state, pltpu.VMEM((phys, blk, blk), F32),
             pltpu.VMEM((regions, slots, blk), F32),
             pltpu.VMEM((regions, slots, blk), F32),
             pltpu.VMEM((slots, blk), F32),
-            pltpu.VMEM((DAV + 1, 8, blk), F32),
-            pltpu.VMEM((DAV + 1, sectors, 8, blk), F32),
+            pltpu.VMEM((16, blk), F32),
+            pltpu.VMEM((sectors, 16, blk), F32),
             dma((slots,)), dma((slots,)), dma((slots,)), dma((slots,)), dma((slots,)),
             dma((2, regions)), dma((2, regions)),
-            dma((DAV + 1, sectors)), dma((DAV + 1, sectors)),
+            dma((sectors,)), dma((sectors,)),
         ],
         compiler_params=pltpu.CompilerParams(collective_id=0, has_side_effects=True),
     )(

time: 65.5 us -> 64.1 us (0.979)
  Pallas kernels: 64.1 us -> 62.6 us
    pallas_call x1, Pallas kernels: 61.3 us -> 59.9 us  [body(): pl.pallas_call(functools.partial(kernel, regions, sectors), out_shape=(ja...]
where the time goes in v1:
time: 64.1 us; the launch traced here: 63.9 us
  Pallas kernels  62.6 us (98%)
  between operations  1.29 us (2%)
    pallas_call x1, Pallas kernels, body(): pl.pallas_call(functools.partial(kernel, regions, sectors), out_shape=(ja...  59.9 us
    pallas_call x1, Pallas kernels, body(): pl.pallas_call(finish, out_shape=(jax.ShapeDtypeStruct((slots, wide, blk)...  2.73 us

profile of v1, /device:TPU:2, one launch (start us, length us, event | category | flops | bytes accessed | tf_op | source)
XLA Modules:
  0.0 63.9 jit_solution(3421528581215683211)
XLA Ops:
  1.3 59.9 %shard_map.94 = (bf16[4,4,128,128]{3,2,1,0:T(8,128)(2,1)}, f32[8,128]{1,0:T(8,128)}) custom-call(bf16[4,512,128]{2,1,0:T(8,128)(2,1)} %bitcast.10, bf16[4,16,128,128]{3,2,1,0:T(8,128)(2,1)} %bitcast.8, bf16[4,16,128,128]{3,2,1,0:T(8,128)(2,1)} %bitcast.9, bf16[256,16]{1,0:T(8,128)(2,1)} %bitcast.11, f32[4,128]{1,0:T(4,128)} %bitcast.12, f32[4,128]{1,0:T(4,128)} %bitcast.13, ...), custom_call_target="tpu_custom_call" | custom-call | tf_op jit(solution)/shard_map/pallas_call | solution.py:377
  61.2 2.7 %shard_map.95 = (bf16[4,512,128]{2,1,0:T(8,128)(2,1)}, f32[4,128,128]{2,1,0:T(8,128)}, f32[1]{0:T(128)}) custom-call(bf16[4,4,128,128]{3,2,1,0:T(8,128)(2,1)} %get-tuple-element.8.state, f32[8,128]{1,0:T(8,128)} %get-tuple-element.9.energy), custom_call_target="tpu_custom_call" | custom-call | tf_op jit(solution)/shard_map/pallas_call | solution.py:412

commit v2 on v1

v2 whole, which is shorter than its diff:
```python
import functools
import math

import jax
import jax.numpy as jnp
from jax import lax
from jax.experimental import pallas as pl
from jax.experimental.pallas import tpu as pltpu
from jax.sharding import PartitionSpec as P

DAV = 2
EPS = 1e-06
MESH = pl.DeviceIdType.MESH
F32 = jnp.float32
BF16 = jnp.bfloat16
STEPS = DAV + 1
TILE = 16


def half_rotation(y, x):
    top = jnp.maximum(jnp.abs(x), jnp.abs(y))
    safe = jnp.where(top > 0, top, 1.0)
    xn, yn = x / safe, y / safe
    h = jnp.sqrt(xn * xn + yn * yn)
    h = jnp.where(top > 0, h, 1.0)
    big = jnp.sqrt(0.5 * (h + jnp.abs(xn)) / h)
    small = jnp.abs(yn) / (2.0 * h * big)
    big = jnp.where(top > 0, big, 1.0)
    small = jnp.where(top > 0, small, 0.0)
    cos_part = jnp.where(x >= 0, big, small)
    sin_size = jnp.where(x >= 0, small, big)
    return cos_part, jnp.where(y > 0, sin_size, -sin_size)


def kernel(
    regions, sectors, start, left, right, operator, decay, energy, live,
    state_out, energy_out,
    start_in, left_in, right_in, lines, spread, flipped, column,
    vector_a, vector_b, inner_a, inner_b, mixed_a, mixed_b, value_a, value_b,
    basis_a, basis_b, norms_a, norms_b, decay_all, energy_all, part, gathered,
    left_send, left_recv, right_sem, start_sem, pre_send, pre_recv, sum_send, sum_recv,
):
    slots, chan, blk, _ = left.shape
    wide = start.shape[1]
    phys = wide // blk
    me, mine = lax.axis_index("region"), lax.axis_index("sector")
    group = TILE // phys
    side = chan * TILE
    pairs = slots // 2
    rounds = pairs * STEPS
    for n in range(slots):
        pltpu.make_async_copy(right.at[n], right_in.at[n], right_sem.at[n]).start()
        pltpu.make_async_copy(start.at[n], start_in.at[n], start_sem.at[n]).start()

    barrier = pltpu.get_barrier_semaphore()
    for k in range(1, regions):
        pl.semaphore_signal(
            barrier, 1, device_id={"region": lax.rem(me + k, regions)}, device_id_type=MESH
        )
    for k in range(1, sectors):
        pl.semaphore_signal(
            barrier, 1, device_id={"sector": lax.rem(mine + k, sectors)}, device_id_type=MESH
        )
    pl.semaphore_wait(barrier, regions + sectors - 2)

    def left_copy(n):
        return pltpu.make_async_remote_copy(
            src_ref=left.at[n], dst_ref=left_in.at[n],
            send_sem=left_send.at[n], recv_sem=left_recv.at[n],
            device_id={"region": lax.rem(me + 1, regions)}, device_id_type=MESH,
        )

    def own_copy(n):
        return pltpu.make_async_copy(left.at[n], left_in.at[n], left_recv.at[n])

    def prefix_copies(k, slot):
        to = {"region": lax.rem(me + k, regions)}
        return [
            pltpu.make_async_remote_copy(
                src_ref=src, dst_ref=dst.at[slot],
                send_sem=pre_send.at[i, k - 1], recv_sem=pre_recv.at[i, k - 1],
                device_id=to, device_id_type=MESH,
            )
            for i, (src, dst) in enumerate(((decay, decay_all), (energy, energy_all)))
        ]

    for k in range(1, regions):
        for copy in prefix_copies(k, me):
            copy.start()

    @pl.when(me < regions - 1)
    def _():
        for n in range(slots):
            left_copy(n).start()

    @pl.when(me == 0)
    def _():
        for n in range(slots):
            own_copy(n).start()

    live_slots = live[...]
    part[...] = jnp.zeros_like(part)

    lines[...] = operator[...].astype(F32)

    def where_one(test):
        return jnp.where(test, 1.0, 0.0).astype(BF16)

    def grid_of(shape):
        return [lax.broadcasted_iota(jnp.int32, shape, i) for i in range(2)]

    def spread_operator(out, swap):
        r, c = grid_of((side, chan * phys))
        u = (r // group) % chan
        if swap:
            u = u + 1 - 2 * (u % 2)
        pick_row = where_one((c // phys == u) & (c % phys == r // (chan * group)))
        r, c = grid_of((chan, side))
        total = jnp.zeros((side, side), F32)
        for t in range(phys):
            tall = jnp.dot(
                pick_row,
                lines[pl.ds(t, chan * phys, stride=phys), :].astype(BF16),
                preferred_element_type=F32,
            ).astype(BF16)
            pick_column = where_one((c // TILE == r) & (c % phys == t))
            total = total + jnp.dot(tall, pick_column, preferred_element_type=F32)
        r, c = grid_of((side, side))
        out[...] = jnp.where(r % group == (c // phys) % group, total, 0.0).astype(BF16)

    spread_operator(spread, False)
    spread_operator(flipped, True)

    def sum8(value):
        return jnp.sum(value.reshape(-1, 8, value.shape[-1]), axis=0)

    def spread_sum(total):
        return jnp.broadcast_to(jnp.sum(total, keepdims=True).reshape(1, 1), (1, blk))

    def length_of(square, whole):
        square = jnp.maximum(square, 1e-10 * whole)
        inverse = jnp.where(square > 0, lax.rsqrt(jnp.where(square > 0, square, 1.0)), 0.0)
        return square * inverse, inverse

    def share_of(value, norm):
        return jnp.where(norm > 0, value / jnp.where(norm > 0, norm, 1.0), 0.0)

    zero = jnp.zeros((8, blk), F32)
    lane = lax.broadcasted_iota(jnp.int32, (1, blk), 1)
    lane8 = lax.broadcasted_iota(jnp.int32, (8, blk), 1)
    chunk = 64

    def open_slot(n, p, vector, basis, norms):
        pltpu.make_async_copy(right.at[n], right_in.at[n], right_sem.at[n]).wait()
        pltpu.make_async_copy(start.at[n], start_in.at[n], start_sem.at[n]).wait()
        alive = jnp.broadcast_to(jnp.where(n < live_slots, 1.0, 0.0), (1, blk)).astype(F32)
        total = zero
        for r in range(0, wide, chunk):
            first = start_in[n, r : r + chunk].astype(F32) * alive
            basis[p, 0, r : r + chunk] = first
            vector[r : r + chunk] = first.astype(BF16)
            total = total + sum8(first * first)
            for i in range(1, STEPS):
                basis[p, i, r : r + chunk] = jnp.zeros((chunk, blk), F32)
        total = spread_sum(total)
        norms[...] = zero
        norms[0:1] = total
        part[STEPS] = jnp.where(lane8 == mine * slots + n, total, part[STEPS])

    def contract(n, vector, inner, mixed):
        half = wide // 2
        low_rows = lax.broadcasted_iota(jnp.int32, (side, 2 * blk), 0) % (2 * group) < group
        for h in range(2):
            rows = vector[h * half : (h + 1) * half]
            for w in range(0, chan, 2):
                side_by_side = jnp.concatenate([right_in[n, w], right_in[n, w + 1]], axis=1)
                inner[h * half : (h + 1) * half, w * blk : (w + 2) * blk] = jnp.dot(
                    rows, side_by_side, preferred_element_type=F32
                ).astype(BF16)
            for q in range(h * half // (4 * TILE), (h + 1) * half // (4 * TILE)):

                def stacked(g):
                    row = (4 * q + g) * TILE
                    return jnp.concatenate(
                        [inner[row : row + TILE, w * blk : (w + 1) * blk] for w in range(chan)], axis=0
                    )

                even = jnp.dot(
                    spread[...], jnp.concatenate([stacked(0), stacked(2)], axis=1),
                    preferred_element_type=F32,
                )
                odd = jnp.dot(
                    flipped[...], jnp.concatenate([stacked(1), stacked(3)], axis=1),
                    preferred_element_type=F32,
                )
                low = jnp.where(low_rows, even, odd)
                high = jnp.where(low_rows, odd, even)
                for s in range(phys):
                    for m in range(chan // 2):
                        row = s * chan * group + m * 2 * group
                        for k, tile in enumerate((low, high)):
                            tile = tile[row : row + 2 * group]
                            if k:
                                tile = pltpu.roll(tile, group, 0)
                            tile = jnp.concatenate([tile[:, :blk], tile[:, blk:]], axis=0).astype(BF16)
                            at = (2 * m + k) * blk + q * TILE
                            mixed[at : at + TILE, s * blk : (s + 1) * blk] = tile

    def close(n, p, j, vector, mixed, value, basis, norms):
        rows = jnp.concatenate([left_in[n, u] for u in range(chan)], axis=1)
        result = jnp.dot(rows, mixed[...], preferred_element_type=F32)
        for s in range(phys):
            value[pl.ds(s, blk, stride=phys), :] = result[:, s * blk : (s + 1) * blk]
        along, whole = [zero] * STEPS, zero
        for r in range(0, wide, chunk):
            image = value[r : r + chunk] + column[n, r : r + chunk] * vector[r : r + chunk].astype(F32)
            value[r : r + chunk] = image
            whole = whole + sum8(image * image)
            for i in range(STEPS):
                along[i] = along[i] + sum8(basis[p, i, r : r + chunk] * image)
        along, whole = [spread_sum(a) for a in along], spread_sum(whole)
        shares = [share_of(a, norms[i : i + 1]) for i, a in enumerate(along)]
        square = whole
        for a, c in zip(along, shares):
            square = square - a * c
        length, inverse = length_of(square, whole)
        cross, norm = [zero] * STEPS, zero
        for r in range(0, wide, chunk):
            bases = [basis[p, i, r : r + chunk] for i in range(STEPS)]
            probe = value[r : r + chunk]
            for c, b in zip(shares, bases):
                probe = probe - c * b
            probe = probe * inverse
            vector[r : r + chunk] = probe.astype(BF16)
            basis[p, j + 1, r : r + chunk] = probe
            norm = norm + sum8(probe * probe)
            for i, b in enumerate(bases):
                cross[i] = cross[i] + sum8(b * probe)
        norm = spread_sum(norm)
        line = lax.broadcasted_iota(jnp.int32, (8, blk), 0)
        norms[...] = jnp.where(line == j + 1, norm, norms[...])
        numbers = [*shares, length, *[spread_sum(c) for c in cross], norm]
        tile = zero
        for i, number in enumerate(numbers):
            tile = jnp.where(line == i, number, tile)
        part[j] = jnp.where(lane8 == mine * slots + n, tile, part[j])

    open_slot(0, 0, vector_a, basis_a, norms_a)
    open_slot(1, 0, vector_b, basis_b, norms_b)
    contract(0, vector_a, inner_a, mixed_a)

    decay_all[me] = decay[...]
    energy_all[me] = energy[...]
    for k in range(1, regions):
        for copy in prefix_copies(k, lax.rem(me + regions - k, regions)):
            copy.wait()
    offsets = jnp.zeros((slots, blk), F32)
    for p in range(regions - 1):
        offsets = jnp.where(p < me, decay_all[p] * offsets + energy_all[p], offsets)
    for n in range(slots):
        turned = jnp.broadcast_to(offsets[n : n + 1], (blk, blk)).T
        for s in range(phys):
            column[n, pl.ds(s, blk, stride=phys), :] = turned

    def turn(i, carry):
        p, j = i // STEPS, i % STEPS
        n = 2 * p
        after = (i + 1) % rounds

        @pl.when(j == 0)
        def _():
            own_copy(n).wait()

        close(n, p, j, vector_a, mixed_a, value_a, basis_a, norms_a)
        contract(n + 1, vector_b, inner_b, mixed_b)

        @pl.when(j == 0)
        def _():
            own_copy(n + 1).wait()

        @pl.when((j == STEPS - 1) & (i + 1 < rounds))
        def _():
            open_slot(n + 2, p + 1, vector_a, basis_a, norms_a)

        close(n + 1, p, j, vector_b, mixed_b, value_b, basis_b, norms_b)
        contract(2 * (after // STEPS), vector_a, inner_a, mixed_a)

        @pl.when((j == STEPS - 1) & (i + 1 < rounds))
        def _():
            open_slot(n + 3, p + 1, vector_b, basis_b, norms_b)

        return carry

    lax.fori_loop(0, rounds, turn, 0)

    gathered[mine] = part[...]

    def copy_of(k, slot):
        return pltpu.make_async_remote_copy(
            src_ref=part, dst_ref=gathered.at[slot],
            send_sem=sum_send.at[k - 1], recv_sem=sum_recv.at[k - 1],
            device_id={"sector": lax.rem(mine + k, sectors)}, device_id_type=MESH,
        )

    for k in range(1, sectors):
        copy_of(k, mine).start()
    for k in range(1, sectors):
        copy_of(k, lax.rem(mine + sectors - k, sectors)).wait()
    table = gathered[0]
    for i in range(1, sectors):
        table = table + gathered[i]
    images = [[table[j, i : i + 1] for i in range(STEPS)] + [None] for j in range(STEPS)]
    gram = {(0, 0): table[STEPS, 0:1]}
    for j in range(STEPS):
        length = table[j, STEPS : STEPS + 1]
        images[j] = [c if i <= j else None for i, c in enumerate(images[j])]
        images[j][j + 1] = length
        for i in range(j + 1):
            gram[i, j + 1] = table[j, STEPS + 1 + i : STEPS + 2 + i]
        gram[j + 1, j + 1] = table[j, 2 * STEPS + 1 : 2 * STEPS + 2]

    def inner(x, y):
        total = jnp.zeros((1, blk), F32)
        for i, xi in enumerate(x):
            for j, yj in enumerate(y):
                if xi is not None and yj is not None:
                    total = total + xi * yj * gram[min(i, j), max(i, j)]
        return jnp.broadcast_to(jnp.sum(total, axis=1, keepdims=True), (1, blk))

    def mix(p, x, q, y):
        def one(a, b):
            if a is None:
                return None if b is None else q * b
            return p * a if b is None else p * a + q * b

        return [one(a, b) for a, b in zip(x, y)]

    unit = jnp.ones((1, blk), F32)
    inverse = lax.rsqrt(inner([unit], [unit]) + EPS)
    current = [inverse * unit, None, None, None]
    applied = [inverse * a if a is not None else None for a in images[0]]
    for _ in range(DAV):
        quotient = inner(current, applied)
        residual = mix(1.0, applied, -quotient, current)
        resid_sq = inner(residual, residual)
        factor = lax.rsqrt(resid_sq + EPS)
        search = [factor * a if a is not None else None for a in residual]
        moved = [None] * (STEPS + 1)
        for a, line in zip(search, images):
            if a is not None:
                moved = mix(1.0, moved, a, line)
        curvature = inner(search, moved)
        cos_part, sin_part = half_rotation(-2.0 * resid_sq * factor, curvature - quotient)
        current = mix(cos_part, current, sin_part, search)
        applied = mix(cos_part, applied, sin_part, moved)
    energy_out[...] = jnp.broadcast_to(inner(current, applied), (8, blk))
    scale = math.sqrt(slots * sectors * blk * phys * blk)

    for n in range(slots):
        here = lane == mine * slots + n
        basis = (basis_a, basis_b)[n % 2]
        factors = [
            jnp.broadcast_to(jnp.sum(jnp.where(here, scale * c, 0.0), axis=1, keepdims=True), (1, blk))
            for c in current[:STEPS]
        ]
        for r in range(0, wide, chunk):
            state = jnp.zeros((chunk, blk), F32)
            for i, c in enumerate(factors):
                state = state + c * basis[n // 2, i, r : r + chunk]
            state_out[n, r : r + chunk] = state.astype(BF16)

    @pl.when(me < regions - 1)
    def _():
        for n in range(slots):
            left_copy(n).wait_send()


def finish(state, energy, out, density, energy_out, rows_buf, density_buf, sems):
    slots, wide, blk = state.shape
    phys = wide // blk
    copies = [pltpu.make_async_copy(state, out, sems.at[slots])]
    copies[0].start()
    for n in range(slots):
        rows_buf[n] = state[n].astype(F32)
        total = jnp.zeros((blk, blk), F32)
        for s in range(phys):
            rows = rows_buf[n, pl.ds(s, blk, stride=phys), :].astype(BF16)
            total = total + lax.dot_general(
                rows, rows, (((1,), (1,)), ((), ())), preferred_element_type=F32
            )
        density_buf[n] = total / (phys * blk)
        copies.append(pltpu.make_async_copy(density_buf.at[n], density.at[n], sems.at[n]))
        copies[-1].start()
    energy_out[0] = energy[0, 0]
    for copy in copies:
        copy.wait()


def body(regions, sectors, start_state, left_env, right_env, mpo_tensor, decay, energy_terms, live_count):
    _, slots, blk, phys, _ = start_state.shape
    chan = left_env.shape[2]
    wide = phys * blk
    side = chan * TILE
    vmem = pl.BlockSpec(memory_space=pltpu.VMEM)
    hbm = pl.BlockSpec(memory_space=pl.ANY)
    smem = pl.BlockSpec(memory_space=pltpu.SMEM)
    dma = pltpu.SemaphoreType.DMA
    twice = lambda *spec: [pltpu.VMEM(*spec)] * 2
    outs = pl.pallas_call(
        functools.partial(kernel, regions, sectors),
        out_shape=(
            jax.ShapeDtypeStruct((slots, wide, blk), BF16),
            jax.ShapeDtypeStruct((8, blk), F32),
        ),
        in_specs=[hbm, hbm, hbm, vmem, vmem, vmem, vmem],
        out_specs=(vmem, vmem),
        scratch_shapes=[
            pltpu.VMEM((slots, wide, blk), BF16),
            pltpu.VMEM((slots, chan, blk, blk), BF16),
            pltpu.VMEM((slots, chan, blk, blk), BF16),
            pltpu.VMEM((chan * phys * phys, chan), F32),
            *twice((side, side), BF16),
            pltpu.VMEM((slots, wide, blk), F32),
            *twice((wide, blk), BF16),
            *twice((wide, chan * blk), BF16),
            *twice((chan * blk, wide), BF16),
            *twice((wide, blk), F32),
            *twice((slots // 2, STEPS + 1, wide, blk), F32),
            *twice((8, blk), F32),
            pltpu.VMEM((regions, slots, blk), F32),
            pltpu.VMEM((regions, slots, blk), F32),
            pltpu.VMEM((STEPS + 1, 8, blk), F32),
            pltpu.VMEM((sectors, STEPS + 1, 8, blk), F32),
            dma((slots,)), dma((slots,)), dma((slots,)), dma((slots,)),
            dma((2, regions)), dma((2, regions)),
            dma((sectors,)), dma((sectors,)),
        ],
        compiler_params=pltpu.CompilerParams(
            collective_id=0, has_side_effects=True, vmem_limit_bytes=48 * 2**20
        ),
    )(
        start_state.reshape(slots, wide, blk), left_env[0], right_env[0],
        mpo_tensor.reshape(chan * phys * phys, chan),
        decay[0], energy_terms[0], live_count,
    )
    state_out, density, energy = pl.pallas_call(
        finish,
        out_shape=(
            jax.ShapeDtypeStruct((slots, wide, blk), BF16),
            jax.ShapeDtypeStruct((slots, blk, blk), F32),
            jax.ShapeDtypeStruct((1,), F32),
        ),
        in_specs=[vmem, vmem],
        out_specs=(hbm, hbm, smem),
        scratch_shapes=[
            pltpu.VMEM((slots, wide, blk), F32),
            pltpu.VMEM((slots, blk, blk), F32),
            dma((slots + 1,)),
        ],
    )(*outs)
    return (
        state_out.reshape(start_state.shape),
        density.reshape(1, slots, blk, blk),
        energy,
    )


def solution(mesh):
    in_specs = (
        P("region", "sector", None, None, None),
        P("region", "sector", None, None, None),
        P("region", "sector", None, None, None),
        P(),
        P("region", "sector", None),
        P("region", "sector", None),
        P("region", "sector"),
    )
    out_specs = (
        P("region", "sector", None, None, None),
        P("region", "sector", None, None),
        P("region"),
    )
    step = functools.partial(body, mesh.shape["region"], mesh.shape["sector"])
    return jax.shard_map(step, mesh=mesh, in_specs=in_specs, out_specs=out_specs, check_vma=False)
```

time: 64.1 us -> 57.3 us (0.89)
  Pallas kernels: 62.6 us -> 47.9 us
  local copies, waits for them, and re-layouts: 0 us -> 7.79 us
    pallas_call x1, Pallas kernels: 59.9 us -> 45.1 us  [body(): pl.pallas_call(functools.partial(kernel, regions, sectors), out_shape=(ja...]
    unnamed x0 -> x16, local copies, waits for them, and re-layouts: none -> 7.79 us
where the time goes in v2:
time: 57.3 us; the launch traced here: 57 us
  Pallas kernels  47.9 us (84%)
  local copies, waits for them, and re-layouts  7.79 us (14%)
  between operations  1.31 us (2%)
    pallas_call x1, Pallas kernels, body(): pl.pallas_call(functools.partial(kernel, regions, sectors), out_shape=(ja...  45.1 us
    unnamed x16, local copies, waits for them, and re-layouts  7.79 us
    pallas_call x1, Pallas kernels, body(): pl.pallas_call(finish, out_shape=(jax.ShapeDtypeStruct((slots, wide, blk)...  2.76 us

profile of v2, /device:TPU:2, one launch (start us, length us, event | category | flops | bytes accessed | tf_op | source)
XLA Modules:
  0.0 57.0 jit_solution(10572868149528645338)
XLA Ops:
  1.3 0.0 copy-start
  1.3 1.6 %copy-done = bf16[1,4,16,128,128]{4,3,2,1,0:T(8,128)(2,1)S(1)} copy-done((bf16[1,4,16,128,128]{4,3,2,1,0:T(8,128)(2,1)S(1)}, bf16[1,4,16,128,128]{4,3,2,1,0:T(8,128)(2,1)}, u32[]{:S(2)}) %copy-start) | copy-done | bytes 2097176
  2.9 0.0 copy-start.1
  2.9 1.6 %copy-done.1 = bf16[1,4,16,128,128]{4,3,2,1,0:T(8,128)(2,1)S(1)} copy-done((bf16[1,4,16,128,128]{4,3,2,1,0:T(8,128)(2,1)S(1)}, bf16[1,4,16,128,128]{4,3,2,1,0:T(8,128)(2,1)}, u32[]{:S(2)}) %copy-start.1) | copy-done | bytes 2097176
  4.5 0.0 copy-start.2
  4.5 1.0 %copy-done.2 = bf16[1,4,128,4,128]{4,3,2,1,0:T(4,128)(2,1)S(1)} copy-done((bf16[1,4,128,4,128]{4,3,2,1,0:T(4,128)(2,1)S(1)}, bf16[1,4,128,4,128]{4,3,2,1,0:T(4,128)(2,1)}, u32[]{:S(2)}) %copy-start.2) | copy-done | bytes 524312
  5.5 0.0 copy-start.4
  5.5 0.8 %copy-done.4 = bf16[16,4,4,16]{3,2,1,0:T(4,128)(2,1)S(1)} copy-done((bf16[16,4,4,16]{3,2,1,0:T(4,128)(2,1)S(1)}, bf16[16,4,4,16]{3,2,1,0:T(4,128)(2,1)}, u32[]{:S(2)}) %copy-start.4) | copy-done | bytes 8216
  6.3 0.0 copy-start.6
  6.3 0.7 %copy-done.6 = f32[1,4,128]{2,1,0:T(4,128)S(1)} copy-done((f32[1,4,128]{2,1,0:T(4,128)S(1)}, f32[1,4,128]{2,1,0:T(4,128)}, u32[]{:S(2)}) %copy-start.6) | copy-done | bytes 2072
  7.0 0.0 copy-start.7
  7.0 0.7 %copy-done.7 = f32[1,4,128]{2,1,0:T(4,128)S(1)} copy-done((f32[1,4,128]{2,1,0:T(4,128)S(1)}, f32[1,4,128]{2,1,0:T(4,128)}, u32[]{:S(2)}) %copy-start.7) | copy-done | bytes 2072
  7.7 45.1 %shard_map.94 = (bf16[4,512,128]{2,1,0:T(8,128)(2,1)S(1)}, f32[8,128]{1,0:T(8,128)S(1)}) custom-call(bf16[4,512,128]{2,1,0:T(8,128)(2,1)S(1)} %bitcast.10, bf16[4,16,128,128]{3,2,1,0:T(8,128)(2,1)S(1)} %bitcast.8, bf16[4,16,128,128]{3,2,1,0:T(8,128)(2,1)S(1)} %bitcast.9, bf16[256,16]{1,0:T(8,128)(2,1)S(1)} %bitcast.11, f32[4,128]{1,0:T(4,128)S(1)} %bitcast.12, ...), custom_call_target="tpu_custom_call" | custom-call | tf_op jit(solution)/shard_map/pallas_call | solution.py:409
  52.8 0.0 copy-start.3
  52.8 0.8 %copy-done.3 = bf16[4,512,128]{2,1,0:T(8,128)(2,1)} copy-done((bf16[4,512,128]{2,1,0:T(8,128)(2,1)}, bf16[4,512,128]{2,1,0:T(8,128)(2,1)S(1)}, u32[]{:S(2)}) %copy-start.3) | copy-done | bytes 524312
  53.6 0.0 copy-start.5
  53.6 0.6 %copy-done.5 = f32[8,128]{1,0:T(8,128)} copy-done((f32[8,128]{1,0:T(8,128)}, f32[8,128]{1,0:T(8,128)S(1)}, u32[]{:S(2)}) %copy-start.5) | copy-done | bytes 4120
  54.2 2.8 %shard_map.95 = (bf16[4,512,128]{2,1,0:T(8,128)(2,1)}, f32[4,128,128]{2,1,0:T(8,128)}, f32[1]{0:T(128)}) custom-call(bf16[4,512,128]{2,1,0:T(8,128)(2,1)} %copy-done.3, f32[8,128]{1,0:T(8,128)} %copy-done.5), custom_call_target="tpu_custom_call" | custom-call | tf_op jit(solution)/shard_map/pallas_call | solution.py:446
Async XLA Ops:
  1.3 1.6 %copy-start = (bf16[1,4,16,128,128]{4,3,2,1,0:T(8,128)(2,1)S(1)}, bf16[1,4,16,128,128]{4,3,2,1,0:T(8,128)(2,1)}, u32[]{:S(2)}) copy-start(bf16[1,4,16,128,128]{4,3,2,1,0:T(8,128)(2,1)} %param.8) | copy-start | bytes 6291460
  2.9 1.6 %copy-start.1 = (bf16[1,4,16,128,128]{4,3,2,1,0:T(8,128)(2,1)S(1)}, bf16[1,4,16,128,128]{4,3,2,1,0:T(8,128)(2,1)}, u32[]{:S(2)}) copy-start(bf16[1,4,16,128,128]{4,3,2,1,0:T(8,128)(2,1)} %param.9) | copy-start | bytes 6291460
  4.5 1.0 %copy-start.2 = (bf16[1,4,128,4,128]{4,3,2,1,0:T(4,128)(2,1)S(1)}, bf16[1,4,128,4,128]{4,3,2,1,0:T(4,128)(2,1)}, u32[]{:S(2)}) copy-start(bf16[1,4,128,4,128]{4,3,2,1,0:T(4,128)(2,1)} %param.7) | copy-start | bytes 1572868
  5.5 0.8 %copy-start.4 = (bf16[16,4,4,16]{3,2,1,0:T(4,128)(2,1)S(1)}, bf16[16,4,4,16]{3,2,1,0:T(4,128)(2,1)}, u32[]{:S(2)}) copy-start(bf16[16,4,4,16]{3,2,1,0:T(4,128)(2,1)} %param.10) | copy-start | bytes 24580
  6.3 0.7 %copy-start.6 = (f32[1,4,128]{2,1,0:T(4,128)S(1)}, f32[1,4,128]{2,1,0:T(4,128)}, u32[]{:S(2)}) copy-start(f32[1,4,128]{2,1,0:T(4,128)} %param.11) | copy-start | bytes 6148
  7.0 0.7 %copy-start.7 = (f32[1,4,128]{2,1,0:T(4,128)S(1)}, f32[1,4,128]{2,1,0:T(4,128)}, u32[]{:S(2)}) copy-start(f32[1,4,128]{2,1,0:T(4,128)} %param.12) | copy-start | bytes 6148
  52.8 0.8 %copy-start.3 = (bf16[4,512,128]{2,1,0:T(8,128)(2,1)}, bf16[4,512,128]{2,1,0:T(8,128)(2,1)S(1)}, u32[]{:S(2)}) copy-start(bf16[4,512,128]{2,1,0:T(8,128)(2,1)S(1)} %get-tuple-element.8.state) | copy-start | bytes 1572868
  53.6 0.6 %copy-start.5 = (f32[8,128]{1,0:T(8,128)}, f32[8,128]{1,0:T(8,128)S(1)}, u32[]{:S(2)}) copy-start(f32[8,128]{1,0:T(8,128)S(1)} %get-tuple-element.9.energy) | copy-start | bytes 12292

commit v3 on v2

--- a/solution.py
+++ b/solution.py
@@ -148,6 +148,7 @@
     zero = jnp.zeros((8, blk), F32)
     lane = lax.broadcasted_iota(jnp.int32, (1, blk), 1)
     lane8 = lax.broadcasted_iota(jnp.int32, (8, blk), 1)
+    line8 = lax.broadcasted_iota(jnp.int32, (8, blk), 0)
     chunk = 64
 
     def open_slot(n, p, vector, basis, norms):
@@ -165,7 +166,7 @@
         total = spread_sum(total)
         norms[...] = zero
         norms[0:1] = total
-        part[STEPS] = jnp.where(lane8 == mine * slots + n, total, part[STEPS])
+        part[...] = jnp.where((line8 == n) & (lane8 == 8 * STEPS), total, part[...])
 
     def contract(n, vector, inner, mixed):
         half = wide // 2
@@ -237,13 +238,12 @@
             for i, b in enumerate(bases):
                 cross[i] = cross[i] + sum8(b * probe)
         norm = spread_sum(norm)
-        line = lax.broadcasted_iota(jnp.int32, (8, blk), 0)
-        norms[...] = jnp.where(line == j + 1, norm, norms[...])
+        norms[...] = jnp.where(line8 == j + 1, norm, norms[...])
         numbers = [*shares, length, *[spread_sum(c) for c in cross], norm]
-        tile = zero
+        row = jnp.zeros((1, blk), F32)
         for i, number in enumerate(numbers):
-            tile = jnp.where(line == i, number, tile)
-        part[j] = jnp.where(lane8 == mine * slots + n, tile, part[j])
+            row = jnp.where(lane == 8 * j + i, number, row)
+        part[...] = jnp.where((line8 == n) & (lane8 // 8 == j), row, part[...])
 
     open_slot(0, 0, vector_a, basis_a, norms_a)
     open_slot(1, 0, vector_b, basis_b, norms_b)
@@ -306,26 +306,25 @@
         copy_of(k, mine).start()
     for k in range(1, sectors):
         copy_of(k, lax.rem(mine + sectors - k, sectors)).wait()
-    table = gathered[0]
-    for i in range(1, sectors):
-        table = table + gathered[i]
-    images = [[table[j, i : i + 1] for i in range(STEPS)] + [None] for j in range(STEPS)]
-    gram = {(0, 0): table[STEPS, 0:1]}
+    many = sectors * 8
+    table = gathered[...].reshape(many, blk).T
+    images = [[table[8 * j + i : 8 * j + i + 1] for i in range(STEPS)] + [None] for j in range(STEPS)]
+    gram = {(0, 0): table[8 * STEPS : 8 * STEPS + 1]}
     for j in range(STEPS):
-        length = table[j, STEPS : STEPS + 1]
+        length = table[8 * j + STEPS : 8 * j + STEPS + 1]
         images[j] = [c if i <= j else None for i, c in enumerate(images[j])]
         images[j][j + 1] = length
         for i in range(j + 1):
-            gram[i, j + 1] = table[j, STEPS + 1 + i : STEPS + 2 + i]
-        gram[j + 1, j + 1] = table[j, 2 * STEPS + 1 : 2 * STEPS + 2]
+            gram[i, j + 1] = table[8 * j + STEPS + 1 + i : 8 * j + STEPS + 2 + i]
+        gram[j + 1, j + 1] = table[8 * j + 2 * STEPS + 1 : 8 * j + 2 * STEPS + 2]
 
     def inner(x, y):
-        total = jnp.zeros((1, blk), F32)
+        total = jnp.zeros((1, many), F32)
         for i, xi in enumerate(x):
             for j, yj in enumerate(y):
                 if xi is not None and yj is not None:
                     total = total + xi * yj * gram[min(i, j), max(i, j)]
-        return jnp.broadcast_to(jnp.sum(total, axis=1, keepdims=True), (1, blk))
+        return jnp.broadcast_to(jnp.sum(total, axis=1, keepdims=True), (1, many))
 
     def mix(p, x, q, y):
         def one(a, b):
@@ -335,7 +334,7 @@
 
         return [one(a, b) for a, b in zip(x, y)]
 
-    unit = jnp.ones((1, blk), F32)
+    unit = jnp.ones((1, many), F32)
     inverse = lax.rsqrt(inner([unit], [unit]) + EPS)
     current = [inverse * unit, None, None, None]
     applied = [inverse * a if a is not None else None for a in images[0]]
@@ -353,11 +352,11 @@
         cos_part, sin_part = half_rotation(-2.0 * resid_sq * factor, curvature - quotient)
         current = mix(cos_part, current, sin_part, search)
         applied = mix(cos_part, applied, sin_part, moved)
-    energy_out[...] = jnp.broadcast_to(inner(current, applied), (8, blk))
+    energy_out[...] = jnp.broadcast_to(inner(current, applied)[:, :1], (8, blk))
     scale = math.sqrt(slots * sectors * blk * phys * blk)
 
     for n in range(slots):
-        here = lane == mine * slots + n
+        here = lax.broadcasted_iota(jnp.int32, (1, many), 1) == mine * 8 + n
         basis = (basis_a, basis_b)[n % 2]
         factors = [
             jnp.broadcast_to(jnp.sum(jnp.where(here, scale * c, 0.0), axis=1, keepdims=True), (1, blk))
@@ -402,7 +401,7 @@
     wide = phys * blk
     side = chan * TILE
     vmem = pl.BlockSpec(memory_space=pltpu.VMEM)
-    hbm = pl.BlockSpec(memory_space=pl.ANY)
+    hbm = pl.BlockSpec(memory_space=pltpu.HBM)
     smem = pl.BlockSpec(memory_space=pltpu.SMEM)
     dma = pltpu.SemaphoreType.DMA
     twice = lambda *spec: [pltpu.VMEM(*spec)] * 2
@@ -429,8 +428,8 @@
             *twice((8, blk), F32),
             pltpu.VMEM((regions, slots, blk), F32),
             pltpu.VMEM((regions, slots, blk), F32),
-            pltpu.VMEM((STEPS + 1, 8, blk), F32),
-            pltpu.VMEM((sectors, STEPS + 1, 8, blk), F32),
+            pltpu.VMEM((8, blk), F32),
+            pltpu.VMEM((sectors, 8, blk), F32),
             dma((slots,)), dma((slots,)), dma((slots,)), dma((slots,)),
             dma((2, regions)), dma((2, regions)),
             dma((sectors,)), dma((sectors,)),

time: 57.3 us -> 57.3 us (level)
  no operation moved by 1% of the time
where the time goes in v3:
time: 57.3 us; the launch traced here: 56.9 us
  Pallas kernels  47.8 us (83%)
  local copies, waits for them, and re-layouts  7.79 us (14%)
  between operations  1.31 us (2%)
    pallas_call x1, Pallas kernels, body(): pl.pallas_call(functools.partial(kernel, regions, sectors), out_shape=(ja...  45.1 us
    unnamed x16, local copies, waits for them, and re-layouts  7.79 us
    pallas_call x1, Pallas kernels, body(): pl.pallas_call(finish, out_shape=(jax.ShapeDtypeStruct((slots, wide, blk)...  2.75 us

profile of v3, /device:TPU:2, one launch (start us, length us, event | category | flops | bytes accessed | tf_op | source)
XLA Modules:
  0.0 56.9 jit_solution(16115802460591895568)
XLA Ops:
  1.3 0.0 copy-start
  1.3 1.6 %copy-done = bf16[1,4,16,128,128]{4,3,2,1,0:T(8,128)(2,1)S(1)} copy-done((bf16[1,4,16,128,128]{4,3,2,1,0:T(8,128)(2,1)S(1)}, bf16[1,4,16,128,128]{4,3,2,1,0:T(8,128)(2,1)}, u32[]{:S(2)}) %copy-start) | copy-done | bytes 2097176
  2.9 0.0 copy-start.1
  2.9 1.6 %copy-done.1 = bf16[1,4,16,128,128]{4,3,2,1,0:T(8,128)(2,1)S(1)} copy-done((bf16[1,4,16,128,128]{4,3,2,1,0:T(8,128)(2,1)S(1)}, bf16[1,4,16,128,128]{4,3,2,1,0:T(8,128)(2,1)}, u32[]{:S(2)}) %copy-start.1) | copy-done | bytes 2097176
  4.5 0.0 copy-start.2
  4.5 1.0 %copy-done.2 = bf16[1,4,128,4,128]{4,3,2,1,0:T(4,128)(2,1)S(1)} copy-done((bf16[1,4,128,4,128]{4,3,2,1,0:T(4,128)(2,1)S(1)}, bf16[1,4,128,4,128]{4,3,2,1,0:T(4,128)(2,1)}, u32[]{:S(2)}) %copy-start.2) | copy-done | bytes 524312
  5.5 0.0 copy-start.4
  5.5 0.8 %copy-done.4 = bf16[16,4,4,16]{3,2,1,0:T(4,128)(2,1)S(1)} copy-done((bf16[16,4,4,16]{3,2,1,0:T(4,128)(2,1)S(1)}, bf16[16,4,4,16]{3,2,1,0:T(4,128)(2,1)}, u32[]{:S(2)}) %copy-start.4) | copy-done | bytes 8216
  6.3 0.0 copy-start.6
  6.3 0.7 %copy-done.6 = f32[1,4,128]{2,1,0:T(4,128)S(1)} copy-done((f32[1,4,128]{2,1,0:T(4,128)S(1)}, f32[1,4,128]{2,1,0:T(4,128)}, u32[]{:S(2)}) %copy-start.6) | copy-done | bytes 2072
  7.0 0.0 copy-start.7
  7.0 0.7 %copy-done.7 = f32[1,4,128]{2,1,0:T(4,128)S(1)} copy-done((f32[1,4,128]{2,1,0:T(4,128)S(1)}, f32[1,4,128]{2,1,0:T(4,128)}, u32[]{:S(2)}) %copy-start.7) | copy-done | bytes 2072
  7.7 45.1 %shard_map.94 = (bf16[4,512,128]{2,1,0:T(8,128)(2,1)S(1)}, f32[8,128]{1,0:T(8,128)S(1)}) custom-call(bf16[4,512,128]{2,1,0:T(8,128)(2,1)S(1)} %bitcast.10, bf16[4,16,128,128]{3,2,1,0:T(8,128)(2,1)S(1)} %bitcast.8, bf16[4,16,128,128]{3,2,1,0:T(8,128)(2,1)S(1)} %bitcast.9, bf16[256,16]{1,0:T(8,128)(2,1)S(1)} %bitcast.11, f32[4,128]{1,0:T(4,128)S(1)} %bitcast.12, ...), custom_call_target="tpu_custom_call" | custom-call | tf_op jit(solution)/shard_map/pallas_call | solution.py:408
  52.8 0.0 copy-start.3
  52.8 0.8 %copy-done.3 = bf16[4,512,128]{2,1,0:T(8,128)(2,1)} copy-done((bf16[4,512,128]{2,1,0:T(8,128)(2,1)}, bf16[4,512,128]{2,1,0:T(8,128)(2,1)S(1)}, u32[]{:S(2)}) %copy-start.3) | copy-done | bytes 524312
  53.6 0.0 copy-start.5
  53.6 0.6 %copy-done.5 = f32[8,128]{1,0:T(8,128)} copy-done((f32[8,128]{1,0:T(8,128)}, f32[8,128]{1,0:T(8,128)S(1)}, u32[]{:S(2)}) %copy-start.5) | copy-done | bytes 4120
  54.2 2.8 %shard_map.95 = (bf16[4,512,128]{2,1,0:T(8,128)(2,1)}, f32[4,128,128]{2,1,0:T(8,128)}, f32[1]{0:T(128)}) custom-call(bf16[4,512,128]{2,1,0:T(8,128)(2,1)} %copy-done.3, f32[8,128]{1,0:T(8,128)} %copy-done.5), custom_call_target="tpu_custom_call" | custom-call | tf_op jit(solution)/shard_map/pallas_call | solution.py:445
Async XLA Ops:
  1.3 1.6 %copy-start = (bf16[1,4,16,128,128]{4,3,2,1,0:T(8,128)(2,1)S(1)}, bf16[1,4,16,128,128]{4,3,2,1,0:T(8,128)(2,1)}, u32[]{:S(2)}) copy-start(bf16[1,4,16,128,128]{4,3,2,1,0:T(8,128)(2,1)} %param.8) | copy-start | bytes 6291460
  2.9 1.6 %copy-start.1 = (bf16[1,4,16,128,128]{4,3,2,1,0:T(8,128)(2,1)S(1)}, bf16[1,4,16,128,128]{4,3,2,1,0:T(8,128)(2,1)}, u32[]{:S(2)}) copy-start(bf16[1,4,16,128,128]{4,3,2,1,0:T(8,128)(2,1)} %param.9) | copy-start | bytes 6291460
  4.5 1.0 %copy-start.2 = (bf16[1,4,128,4,128]{4,3,2,1,0:T(4,128)(2,1)S(1)}, bf16[1,4,128,4,128]{4,3,2,1,0:T(4,128)(2,1)}, u32[]{:S(2)}) copy-start(bf16[1,4,128,4,128]{4,3,2,1,0:T(4,128)(2,1)} %param.7) | copy-start | bytes 1572868
  5.5 0.8 %copy-start.4 = (bf16[16,4,4,16]{3,2,1,0:T(4,128)(2,1)S(1)}, bf16[16,4,4,16]{3,2,1,0:T(4,128)(2,1)}, u32[]{:S(2)}) copy-start(bf16[16,4,4,16]{3,2,1,0:T(4,128)(2,1)} %param.10) | copy-start | bytes 24580
  6.3 0.7 %copy-start.6 = (f32[1,4,128]{2,1,0:T(4,128)S(1)}, f32[1,4,128]{2,1,0:T(4,128)}, u32[]{:S(2)}) copy-start(f32[1,4,128]{2,1,0:T(4,128)} %param.11) | copy-start | bytes 6148
  7.0 0.7 %copy-start.7 = (f32[1,4,128]{2,1,0:T(4,128)S(1)}, f32[1,4,128]{2,1,0:T(4,128)}, u32[]{:S(2)}) copy-start(f32[1,4,128]{2,1,0:T(4,128)} %param.12) | copy-start | bytes 6148
  52.8 0.8 %copy-start.3 = (bf16[4,512,128]{2,1,0:T(8,128)(2,1)}, bf16[4,512,128]{2,1,0:T(8,128)(2,1)S(1)}, u32[]{:S(2)}) copy-start(bf16[4,512,128]{2,1,0:T(8,128)(2,1)S(1)} %get-tuple-element.8.state) | copy-start | bytes 1572868
  53.6 0.6 %copy-start.5 = (f32[8,128]{1,0:T(8,128)}, f32[8,128]{1,0:T(8,128)S(1)}, u32[]{:S(2)}) copy-start(f32[8,128]{1,0:T(8,128)S(1)} %get-tuple-element.9.energy) | copy-start | bytes 12292

commit v4 on v3

--- a/solution.py
+++ b/solution.py
@@ -37,7 +37,7 @@
     state_out, energy_out,
     start_in, left_in, right_in, lines, spread, flipped, column,
     vector_a, vector_b, inner_a, inner_b, mixed_a, mixed_b, value_a, value_b,
-    basis_a, basis_b, norms_a, norms_b, decay_all, energy_all, part, gathered,
+    basis, norms, decay_all, energy_all, part, gathered,
     left_send, left_recv, right_sem, start_sem, pre_send, pre_recv, sum_send, sum_recv,
 ):
     slots, chan, blk, _ = left.shape
@@ -46,8 +46,10 @@
     me, mine = lax.axis_index("region"), lax.axis_index("sector")
     group = TILE // phys
     side = chan * TILE
-    pairs = slots // 2
-    rounds = pairs * STEPS
+    here_zero = me // regions
+    crossing = (me > 0) & (me % 2 == 0)
+    rounds = jnp.where(crossing, 0, slots // 2 * STEPS)
+    singles = jnp.where(crossing, slots, 0)
     for n in range(slots):
         pltpu.make_async_copy(right.at[n], right_in.at[n], right_sem.at[n]).start()
         pltpu.make_async_copy(start.at[n], start_in.at[n], start_sem.at[n]).start()
@@ -151,103 +153,161 @@
     line8 = lax.broadcasted_iota(jnp.int32, (8, blk), 0)
     chunk = 64
 
-    def open_slot(n, p, vector, basis, norms):
+    def open_slot(n):
         pltpu.make_async_copy(right.at[n], right_in.at[n], right_sem.at[n]).wait()
         pltpu.make_async_copy(start.at[n], start_in.at[n], start_sem.at[n]).wait()
         alive = jnp.broadcast_to(jnp.where(n < live_slots, 1.0, 0.0), (1, blk)).astype(F32)
         total = zero
         for r in range(0, wide, chunk):
             first = start_in[n, r : r + chunk].astype(F32) * alive
-            basis[p, 0, r : r + chunk] = first
-            vector[r : r + chunk] = first.astype(BF16)
+            basis[n, 0, r : r + chunk] = first
+            vector_a[n, r : r + chunk] = first.astype(BF16)
+            vector_b[n, r : r + chunk] = first.astype(BF16)
             total = total + sum8(first * first)
             for i in range(1, STEPS):
-                basis[p, i, r : r + chunk] = jnp.zeros((chunk, blk), F32)
+                basis[n, i, r : r + chunk] = jnp.zeros((chunk, blk), F32)
         total = spread_sum(total)
-        norms[...] = zero
-        norms[0:1] = total
+        norms[n] = jnp.where(line8 == 0, total, 0.0)
         part[...] = jnp.where((line8 == n) & (lane8 == 8 * STEPS), total, part[...])
+
+    low_rows = lax.broadcasted_iota(jnp.int32, (side, 2 * blk), 0) % (2 * group) < group
 
     def contract(n, vector, inner, mixed):
         half = wide // 2
-        low_rows = lax.broadcasted_iota(jnp.int32, (side, 2 * blk), 0) % (2 * group) < group
-        for h in range(2):
-            rows = vector[h * half : (h + 1) * half]
-            for w in range(0, chan, 2):
-                side_by_side = jnp.concatenate([right_in[n, w], right_in[n, w + 1]], axis=1)
-                inner[h * half : (h + 1) * half, w * blk : (w + 2) * blk] = jnp.dot(
-                    rows, side_by_side, preferred_element_type=F32
-                ).astype(BF16)
-            for q in range(h * half // (4 * TILE), (h + 1) * half // (4 * TILE)):
-
-                def stacked(g):
-                    row = (4 * q + g) * TILE
-                    return jnp.concatenate(
-                        [inner[row : row + TILE, w * blk : (w + 1) * blk] for w in range(chan)], axis=0
-                    )
-
-                even = jnp.dot(
-                    spread[...], jnp.concatenate([stacked(0), stacked(2)], axis=1),
-                    preferred_element_type=F32,
+
+        def right_part(h, w):
+            side_by_side = jnp.concatenate([right_in[n, w], right_in[n, w + 1]], axis=1)
+            inner[h * half : (h + 1) * half, w * blk : (w + 2) * blk] = jnp.dot(
+                vector[n, h * half : (h + 1) * half], side_by_side, preferred_element_type=F32
+            ).astype(BF16)
+
+        def operator_part(q):
+            def stacked(g):
+                row = (4 * q + g) * TILE
+                return jnp.concatenate(
+                    [inner[row : row + TILE, w * blk : (w + 1) * blk] for w in range(chan)], axis=0
                 )
-                odd = jnp.dot(
-                    flipped[...], jnp.concatenate([stacked(1), stacked(3)], axis=1),
-                    preferred_element_type=F32,
-                )
-                low = jnp.where(low_rows, even, odd)
-                high = jnp.where(low_rows, odd, even)
-                for s in range(phys):
-                    for m in range(chan // 2):
-                        row = s * chan * group + m * 2 * group
-                        for k, tile in enumerate((low, high)):
-                            tile = tile[row : row + 2 * group]
-                            if k:
-                                tile = pltpu.roll(tile, group, 0)
-                            tile = jnp.concatenate([tile[:, :blk], tile[:, blk:]], axis=0).astype(BF16)
-                            at = (2 * m + k) * blk + q * TILE
-                            mixed[at : at + TILE, s * blk : (s + 1) * blk] = tile
-
-    def close(n, p, j, vector, mixed, value, basis, norms):
-        rows = jnp.concatenate([left_in[n, u] for u in range(chan)], axis=1)
-        result = jnp.dot(rows, mixed[...], preferred_element_type=F32)
-        for s in range(phys):
-            value[pl.ds(s, blk, stride=phys), :] = result[:, s * blk : (s + 1) * blk]
-        along, whole = [zero] * STEPS, zero
-        for r in range(0, wide, chunk):
-            image = value[r : r + chunk] + column[n, r : r + chunk] * vector[r : r + chunk].astype(F32)
-            value[r : r + chunk] = image
-            whole = whole + sum8(image * image)
-            for i in range(STEPS):
-                along[i] = along[i] + sum8(basis[p, i, r : r + chunk] * image)
-        along, whole = [spread_sum(a) for a in along], spread_sum(whole)
-        shares = [share_of(a, norms[i : i + 1]) for i, a in enumerate(along)]
-        square = whole
-        for a, c in zip(along, shares):
-            square = square - a * c
-        length, inverse = length_of(square, whole)
-        cross, norm = [zero] * STEPS, zero
-        for r in range(0, wide, chunk):
-            bases = [basis[p, i, r : r + chunk] for i in range(STEPS)]
-            probe = value[r : r + chunk]
-            for c, b in zip(shares, bases):
-                probe = probe - c * b
-            probe = probe * inverse
-            vector[r : r + chunk] = probe.astype(BF16)
-            basis[p, j + 1, r : r + chunk] = probe
-            norm = norm + sum8(probe * probe)
-            for i, b in enumerate(bases):
-                cross[i] = cross[i] + sum8(b * probe)
-        norm = spread_sum(norm)
-        norms[...] = jnp.where(line8 == j + 1, norm, norms[...])
-        numbers = [*shares, length, *[spread_sum(c) for c in cross], norm]
-        row = jnp.zeros((1, blk), F32)
-        for i, number in enumerate(numbers):
-            row = jnp.where(lane == 8 * j + i, number, row)
-        part[...] = jnp.where((line8 == n) & (lane8 // 8 == j), row, part[...])
-
-    open_slot(0, 0, vector_a, basis_a, norms_a)
-    open_slot(1, 0, vector_b, basis_b, norms_b)
-    contract(0, vector_a, inner_a, mixed_a)
+
+            even = jnp.dot(
+                spread[...], jnp.concatenate([stacked(0), stacked(2)], axis=1),
+                preferred_element_type=F32,
+            )
+            odd = jnp.dot(
+                flipped[...], jnp.concatenate([stacked(1), stacked(3)], axis=1),
+                preferred_element_type=F32,
+            )
+            low = jnp.where(low_rows, even, odd)
+            high = jnp.where(low_rows, odd, even)
+            for s in range(phys):
+                for m in range(chan // 2):
+                    row = s * chan * group + m * 2 * group
+                    for k, tile in enumerate((low, high)):
+                        tile = tile[row : row + 2 * group]
+                        if k:
+                            tile = pltpu.roll(tile, group, 0)
+                        tile = jnp.concatenate([tile[:, :blk], tile[:, blk:]], axis=0).astype(BF16)
+                        at = (2 * m + k) * blk + q * TILE
+                        mixed[at : at + TILE, s * blk : (s + 1) * blk] = tile
+
+        rights = [functools.partial(right_part, h, w) for h in range(2) for w in range(0, chan, 2)]
+        return rights, [functools.partial(operator_part, q) for q in range(wide // (4 * TILE))]
+
+    def close(n, j, vector, mixed, value):
+        held = {"along": [zero] * STEPS, "whole": zero, "norm": zero}
+
+        def left_part():
+            rows = jnp.concatenate([left_in[n, u] for u in range(chan)], axis=1)
+            result = jnp.dot(rows, mixed[...], preferred_element_type=F32)
+            for s in range(phys):
+                value[0, pl.ds(s, blk, stride=phys), :] = result[:, s * blk : (s + 1) * blk]
+
+        def image_part(r):
+            image = value[0, r : r + chunk] + column[n, r : r + chunk] * vector[n, r : r + chunk].astype(F32)
+            value[0, r : r + chunk] = image
+            held["whole"] = held["whole"] + sum8(image * image)
+            held["along"] = [
+                a + sum8(basis[n, i, r : r + chunk] * image) for i, a in enumerate(held["along"])
+            ]
+
+        def number_part():
+            along, whole = [spread_sum(a) for a in held["along"]], spread_sum(held["whole"])
+            shares = [share_of(a, norms[n, i : i + 1]) for i, a in enumerate(along)]
+            square = whole
+            for a, c in zip(along, shares):
+                square = square - a * c
+            held["shares"] = shares
+            held["length"], held["inverse"] = length_of(square, whole)
+
+        def probe_part(r):
+            probe = value[here_zero, r : r + chunk]
+            for i, c in enumerate(held["shares"]):
+                probe = probe - c * basis[n + here_zero, i, r : r + chunk]
+            probe = probe * held["inverse"]
+            vector[n, r : r + chunk] = probe.astype(BF16)
+            basis[n, j + 1, r : r + chunk] = probe
+            held["norm"] = held["norm"] + sum8(probe * probe)
+
+        def record_part():
+            norm = spread_sum(held["norm"])
+            norms[n] = jnp.where(line8 == j + 1, norm, norms[n])
+            row = jnp.zeros((1, blk), F32)
+            for i, number in enumerate([*held["shares"], held["length"], norm]):
+                row = jnp.where(lane == 8 * j + i, number, row)
+            part[...] = jnp.where((line8 == n) & (lane8 // 8 == j), row, part[...])
+
+        images = [functools.partial(image_part, r) for r in range(0, wide, chunk)]
+        probes = [functools.partial(probe_part, r) for r in range(0, wide, chunk)]
+        return left_part, images, number_part, probes, record_part
+
+    def run(parts):
+        for one in parts:
+            one()
+
+    def beside(closing, contracting):
+        left_part, images, number_part, probes, record_part = closing
+        rights, operators = contracting
+        run(rights[:4])
+        left_part()
+        run(rights[4:8])
+        for k, one in enumerate(images):
+            one()
+            run(rights[8 + k : 9 + k])
+        number_part()
+        operators[0]()
+        operators[1]()
+        for k, one in enumerate(probes):
+            one()
+            if k % 2:
+                run(operators[2 + k // 2 : 3 + k // 2])
+        run(operators[6:])
+        record_part()
+
+    def before(closing, contracting):
+        left_part, images, number_part, probes, record_part = closing
+        rights, operators = contracting
+        left_part()
+        run(images)
+        number_part()
+        run(probes[:4])
+        for k, one in enumerate(probes[4:]):
+            run(rights[2 * k : 2 * k + 2])
+            one()
+        run(rights[8:])
+        record_part()
+        run(operators)
+
+    def alone(closing):
+        left_part, images, number_part, probes, record_part = closing
+        left_part()
+        run(images)
+        number_part()
+        run(probes)
+        record_part()
+
+    for n in range(slots):
+        open_slot(n)
+    for parts in contract(0, vector_a, inner_a, mixed_a):
+        run(parts)
 
     decay_all[me] = decay[...]
     energy_all[me] = energy[...]
@@ -262,36 +322,43 @@
         for s in range(phys):
             column[n, pl.ds(s, blk, stride=phys), :] = turned
 
-    def turn(i, carry):
-        p, j = i // STEPS, i % STEPS
-        n = 2 * p
-        after = (i + 1) % rounds
-
-        @pl.when(j == 0)
+    @pl.when(jnp.logical_not(crossing))
+    def _():
+        for n in range(slots):
+            own_copy(n).wait()
+
+    def both(i, carry):
+        n, j = i // STEPS * 2, i % STEPS
+        after = (i + 1) % (slots // 2 * STEPS)
+        beside(close(n, j, vector_a, mixed_a, value_a), contract(n + 1, vector_b, inner_b, mixed_b))
+        beside(
+            close(n + 1, j, vector_b, mixed_b, value_b),
+            contract(after // STEPS * 2, vector_a, inner_a, mixed_a),
+        )
+        return carry
+
+    lax.fori_loop(0, rounds, both, 0)
+
+    def single(n, carry):
+        own_copy(n).wait()
+        chain = vector_b, inner_b, mixed_b
+        before(close(n, 0, vector_b, mixed_a, value_b), contract(n, *chain))
+        before(close(n, 1, vector_b, mixed_b, value_b), contract(n, *chain))
+
+        def last():
+            return close(n, STEPS - 1, vector_b, mixed_b, value_b)
+
+        @pl.when(n < slots - 1)
         def _():
-            own_copy(n).wait()
-
-        close(n, p, j, vector_a, mixed_a, value_a, basis_a, norms_a)
-        contract(n + 1, vector_b, inner_b, mixed_b)
-
-        @pl.when(j == 0)
+            beside(last(), contract(n + 1, vector_a, inner_a, mixed_a))
+
+        @pl.when(n == slots - 1)
         def _():
-            own_copy(n + 1).wait()
-
-        @pl.when((j == STEPS - 1) & (i + 1 < rounds))
-        def _():
-            open_slot(n + 2, p + 1, vector_a, basis_a, norms_a)
-
-        close(n + 1, p, j, vector_b, mixed_b, value_b, basis_b, norms_b)
-        contract(2 * (after // STEPS), vector_a, inner_a, mixed_a)
-
-        @pl.when((j == STEPS - 1) & (i + 1 < rounds))
-        def _():
-            open_slot(n + 3, p + 1, vector_b, basis_b, norms_b)
+            alone(last())
 
         return carry
 
-    lax.fori_loop(0, rounds, turn, 0)
+    lax.fori_loop(0, singles, single, 0)
 
     gathered[mine] = part[...]
 
@@ -309,21 +376,18 @@
     many = sectors * 8
     table = gathered[...].reshape(many, blk).T
     images = [[table[8 * j + i : 8 * j + i + 1] for i in range(STEPS)] + [None] for j in range(STEPS)]
-    gram = {(0, 0): table[8 * STEPS : 8 * STEPS + 1]}
+    gram = {0: table[8 * STEPS : 8 * STEPS + 1]}
     for j in range(STEPS):
         length = table[8 * j + STEPS : 8 * j + STEPS + 1]
         images[j] = [c if i <= j else None for i, c in enumerate(images[j])]
         images[j][j + 1] = length
-        for i in range(j + 1):
-            gram[i, j + 1] = table[8 * j + STEPS + 1 + i : 8 * j + STEPS + 2 + i]
-        gram[j + 1, j + 1] = table[8 * j + 2 * STEPS + 1 : 8 * j + 2 * STEPS + 2]
+        gram[j + 1] = table[8 * j + STEPS + 1 : 8 * j + STEPS + 2]
 
     def inner(x, y):
         total = jnp.zeros((1, many), F32)
-        for i, xi in enumerate(x):
-            for j, yj in enumerate(y):
-                if xi is not None and yj is not None:
-                    total = total + xi * yj * gram[min(i, j), max(i, j)]
+        for i, (xi, yi) in enumerate(zip(x, y)):
+            if xi is not None and yi is not None:
+                total = total + xi * yi * gram[i]
         return jnp.broadcast_to(jnp.sum(total, axis=1, keepdims=True), (1, many))
 
     def mix(p, x, q, y):
@@ -335,7 +399,7 @@
         return [one(a, b) for a, b in zip(x, y)]
 
     unit = jnp.ones((1, many), F32)
-    inverse = lax.rsqrt(inner([unit], [unit]) + EPS)
+    inverse = lax.rsqrt(inner([unit] + [None] * STEPS, [unit] + [None] * STEPS) + EPS)
     current = [inverse * unit, None, None, None]
     applied = [inverse * a if a is not None else None for a in images[0]]
     for _ in range(DAV):
@@ -357,7 +421,6 @@
 
     for n in range(slots):
         here = lax.broadcasted_iota(jnp.int32, (1, many), 1) == mine * 8 + n
-        basis = (basis_a, basis_b)[n % 2]
         factors = [
             jnp.broadcast_to(jnp.sum(jnp.where(here, scale * c, 0.0), axis=1, keepdims=True), (1, blk))
             for c in current[:STEPS]
@@ -365,7 +428,7 @@
         for r in range(0, wide, chunk):
             state = jnp.zeros((chunk, blk), F32)
             for i, c in enumerate(factors):
-                state = state + c * basis[n // 2, i, r : r + chunk]
+                state = state + c * basis[n, i, r : r + chunk]
             state_out[n, r : r + chunk] = state.astype(BF16)
 
     @pl.when(me < regions - 1)
@@ -420,12 +483,12 @@
             pltpu.VMEM((chan * phys * phys, chan), F32),
             *twice((side, side), BF16),
             pltpu.VMEM((slots, wide, blk), F32),
-            *twice((wide, blk), BF16),
+            *twice((slots, wide, blk), BF16),
             *twice((wide, chan * blk), BF16),
             *twice((chan * blk, wide), BF16),
-            *twice((wide, blk), F32),
-            *twice((slots // 2, STEPS + 1, wide, blk), F32),
-            *twice((8, blk), F32),
+            *twice((1, wide, blk), F32),
+            pltpu.VMEM((slots, STEPS + 1, wide, blk), F32),
+            pltpu.VMEM((slots, 8, blk), F32),
             pltpu.VMEM((regions, slots, blk), F32),
             pltpu.VMEM((regions, slots, blk), F32),
             pltpu.VMEM((8, blk), F32),
@@ -435,7 +498,7 @@
             dma((sectors,)), dma((sectors,)),
         ],
         compiler_params=pltpu.CompilerParams(
-            collective_id=0, has_side_effects=True, vmem_limit_bytes=48 * 2**20
+            collective_id=0, has_side_effects=True, vmem_limit_bytes=60 * 2**20
         ),
     )(
         start_state.reshape(slots, wide, blk), left_env[0], right_env[0],

time: 57.3 us -> 44.2 us (0.77)
  local copies, waits for them, and re-layouts: 7.79 us -> 0 us
  Pallas kernels: 47.8 us -> 42.7 us
    unnamed x16 -> x0, local copies, waits for them, and re-layouts: 7.79 us -> none
    pallas_call x1, Pallas kernels: 45.1 us -> 40 us  [body(): pl.pallas_call(functools.partial(kernel, regions, sectors), out_shape=(ja...]
where the time goes in v4:
time: 44.2 us; the launch traced here: 44 us
  Pallas kernels  42.7 us (97%)
  between operations  1.29 us (3%)
    pallas_call x1, Pallas kernels, body(): pl.pallas_call(functools.partial(kernel, regions, sectors), out_shape=(ja...  40 us
    pallas_call x1, Pallas kernels, body(): pl.pallas_call(finish, out_shape=(jax.ShapeDtypeStruct((slots, wide, blk)...  2.75 us

profile of v4, /device:TPU:2, one launch (start us, length us, event | category | flops | bytes accessed | tf_op | source)
XLA Modules:
  0.0 44.0 jit_solution(12915312795593760872)
XLA Ops:
  1.3 40.0 %shard_map.94 = (bf16[4,512,128]{2,1,0:T(8,128)(2,1)}, f32[8,128]{1,0:T(8,128)}) custom-call(bf16[4,512,128]{2,1,0:T(8,128)(2,1)} %bitcast.10, bf16[4,16,128,128]{3,2,1,0:T(8,128)(2,1)} %bitcast.8, bf16[4,16,128,128]{3,2,1,0:T(8,128)(2,1)} %bitcast.9, bf16[256,16]{1,0:T(8,128)(2,1)} %bitcast.11, f32[4,128]{1,0:T(4,128)} %bitcast.12, f32[4,128]{1,0:T(4,128)} %bitcast.13, ...), custom_call_target="tpu_custom_call" | custom-call | tf_op jit(solution)/shard_map/pallas_call | solution.py:471
  41.2 2.8 %shard_map.95 = (bf16[4,512,128]{2,1,0:T(8,128)(2,1)}, f32[4,128,128]{2,1,0:T(8,128)}, f32[1]{0:T(128)}) custom-call(bf16[4,512,128]{2,1,0:T(8,128)(2,1)} %get-tuple-element.8.state, f32[8,128]{1,0:T(8,128)} %get-tuple-element.9.energy), custom_call_target="tpu_custom_call" | custom-call | tf_op jit(solution)/shard_map/pallas_call | solution.py:508

commit v5 on v4

--- a/solution.py
+++ b/solution.py
@@ -35,10 +35,10 @@
 def kernel(
     regions, sectors, start, left, right, operator, decay, energy, live,
     state_out, energy_out,
-    start_in, left_in, right_in, lines, spread, flipped, column,
+    operator_in, live_in, state_buf, energy_buf, start_in, left_in, right_in, lines, spread, flipped, column,
     vector_a, vector_b, inner_a, inner_b, mixed_a, mixed_b, value_a, value_b,
     basis, norms, decay_all, energy_all, part, gathered,
-    left_send, left_recv, right_sem, start_sem, pre_send, pre_recv, sum_send, sum_recv,
+    left_send, left_recv, right_sem, start_sem, small_sem, out_sem, pre_send, pre_recv, sum_send, sum_recv,
 ):
     slots, chan, blk, _ = left.shape
     wide = start.shape[1]
@@ -50,10 +50,6 @@
     crossing = (me > 0) & (me % 2 == 0)
     rounds = jnp.where(crossing, 0, slots // 2 * STEPS)
     singles = jnp.where(crossing, slots, 0)
-    for n in range(slots):
-        pltpu.make_async_copy(right.at[n], right_in.at[n], right_sem.at[n]).start()
-        pltpu.make_async_copy(start.at[n], start_in.at[n], start_sem.at[n]).start()
-
     barrier = pltpu.get_barrier_semaphore()
     for k in range(1, regions):
         pl.semaphore_signal(
@@ -63,6 +59,17 @@
         pl.semaphore_signal(
             barrier, 1, device_id={"sector": lax.rem(mine + k, sectors)}, device_id_type=MESH
         )
+    small = [
+        pltpu.make_async_copy(src, dst, small_sem.at[i])
+        for i, (src, dst) in enumerate((
+            (operator, operator_in), (live, live_in), (decay, decay_all.at[me]), (energy, energy_all.at[me]),
+        ))
+    ]
+    for copy in small:
+        copy.start()
+    for n in range(slots):
+        pltpu.make_async_copy(right.at[n], right_in.at[n], right_sem.at[n]).start()
+        pltpu.make_async_copy(start.at[n], start_in.at[n], start_sem.at[n]).start()
     pl.semaphore_wait(barrier, regions + sectors - 2)
 
     def left_copy(n):
@@ -87,8 +94,11 @@
         ]
 
     for k in range(1, regions):
-        for copy in prefix_copies(k, me):
-            copy.start()
+
+        @pl.when(me + k < regions)
+        def _():
+            for copy in prefix_copies(k, me):
+                copy.start()
 
     @pl.when(me < regions - 1)
     def _():
@@ -100,10 +110,12 @@
         for n in range(slots):
             own_copy(n).start()
 
-    live_slots = live[...]
+    for copy in small:
+        copy.wait()
+    live_slots = live_in[...]
     part[...] = jnp.zeros_like(part)
 
-    lines[...] = operator[...].astype(F32)
+    lines[...] = operator_in[...].astype(F32)
 
     def where_one(test):
         return jnp.where(test, 1.0, 0.0).astype(BF16)
@@ -212,7 +224,7 @@
         rights = [functools.partial(right_part, h, w) for h in range(2) for w in range(0, chan, 2)]
         return rights, [functools.partial(operator_part, q) for q in range(wide // (4 * TILE))]
 
-    def close(n, j, vector, mixed, value):
+    def close(n, j, vector, mixed, value, final=False):
         held = {"along": [zero] * STEPS, "whole": zero, "norm": zero}
 
         def left_part():
@@ -248,15 +260,18 @@
             held["norm"] = held["norm"] + sum8(probe * probe)
 
         def record_part():
-            norm = spread_sum(held["norm"])
-            norms[n] = jnp.where(line8 == j + 1, norm, norms[n])
+            numbers = [*held["shares"]]
+            if not final:
+                norm = spread_sum(held["norm"])
+                norms[n] = jnp.where(line8 == j + 1, norm, norms[n])
+                numbers += [held["length"], norm]
             row = jnp.zeros((1, blk), F32)
-            for i, number in enumerate([*held["shares"], held["length"], norm]):
+            for i, number in enumerate(numbers):
                 row = jnp.where(lane == 8 * j + i, number, row)
             part[...] = jnp.where((line8 == n) & (lane8 // 8 == j), row, part[...])
 
         images = [functools.partial(image_part, r) for r in range(0, wide, chunk)]
-        probes = [functools.partial(probe_part, r) for r in range(0, wide, chunk)]
+        probes = [] if final else [functools.partial(probe_part, r) for r in range(0, wide, chunk)]
         return left_part, images, number_part, probes, record_part
 
     def run(parts):
@@ -275,12 +290,15 @@
         number_part()
         operators[0]()
         operators[1]()
+        if not probes:
+            record_part()
         for k, one in enumerate(probes):
             one()
             if k % 2:
                 run(operators[2 + k // 2 : 3 + k // 2])
-        run(operators[6:])
-        record_part()
+        run(operators[6 if probes else 2 :])
+        if probes:
+            record_part()
 
     def before(closing, contracting):
         left_part, images, number_part, probes, record_part = closing
@@ -309,11 +327,18 @@
     for parts in contract(0, vector_a, inner_a, mixed_a):
         run(parts)
 
-    decay_all[me] = decay[...]
-    energy_all[me] = energy[...]
     for k in range(1, regions):
-        for copy in prefix_copies(k, lax.rem(me + regions - k, regions)):
-            copy.wait()
+
+        @pl.when(me + k < regions)
+        def _():
+            for copy in prefix_copies(k, me):
+                copy.wait_send()
+
+        @pl.when(me >= k)
+        def _():
+            for copy in prefix_copies(k, lax.rem(me + regions - k, regions)):
+                copy.wait_recv()
+
     offsets = jnp.zeros((slots, blk), F32)
     for p in range(regions - 1):
         offsets = jnp.where(p < me, decay_all[p] * offsets + energy_all[p], offsets)
@@ -346,7 +371,7 @@
         before(close(n, 1, vector_b, mixed_b, value_b), contract(n, *chain))
 
         def last():
-            return close(n, STEPS - 1, vector_b, mixed_b, value_b)
+            return close(n, STEPS - 1, vector_b, mixed_b, value_b, final=True)
 
         @pl.when(n < slots - 1)
         def _():
@@ -369,7 +394,7 @@
             device_id={"sector": lax.rem(mine + k, sectors)}, device_id_type=MESH,
         )
 
-    for k in range(1, sectors):
+    for k in sorted(range(1, sectors), key=lambda k: abs(2 * k - sectors)):
         copy_of(k, mine).start()
     for k in range(1, sectors):
         copy_of(k, lax.rem(mine + sectors - k, sectors)).wait()
@@ -416,9 +441,11 @@
         cos_part, sin_part = half_rotation(-2.0 * resid_sq * factor, curvature - quotient)
         current = mix(cos_part, current, sin_part, search)
         applied = mix(cos_part, applied, sin_part, moved)
-    energy_out[...] = jnp.broadcast_to(inner(current, applied)[:, :1], (8, blk))
+    energy_buf[...] = jnp.broadcast_to(inner(current, applied)[:, :1], (8, blk))
     scale = math.sqrt(slots * sectors * blk * phys * blk)
 
+    copies = [pltpu.make_async_copy(energy_buf, energy_out, out_sem.at[slots])]
+    copies[0].start()
     for n in range(slots):
         here = lax.broadcasted_iota(jnp.int32, (1, many), 1) == mine * 8 + n
         factors = [
@@ -429,7 +456,11 @@
             state = jnp.zeros((chunk, blk), F32)
             for i, c in enumerate(factors):
                 state = state + c * basis[n, i, r : r + chunk]
-            state_out[n, r : r + chunk] = state.astype(BF16)
+            state_buf[n, r : r + chunk] = state.astype(BF16)
+        copies.append(pltpu.make_async_copy(state_buf.at[n], state_out.at[n], out_sem.at[n]))
+        copies[-1].start()
+    for copy in copies:
+        copy.wait()
 
     @pl.when(me < regions - 1)
     def _():
@@ -437,11 +468,16 @@
             left_copy(n).wait_send()
 
 
-def finish(state, energy, out, density, energy_out, rows_buf, density_buf, sems):
+def finish(state, energy, out, density, energy_out, rows_buf, density_buf, energy_buf, sems):
     slots, wide, blk = state.shape
     phys = wide // blk
-    copies = [pltpu.make_async_copy(state, out, sems.at[slots])]
-    copies[0].start()
+    energy_buf[0] = energy[0, 0]
+    copies = [
+        pltpu.make_async_copy(state, out, sems.at[slots]),
+        pltpu.make_async_copy(energy_buf, energy_out, sems.at[slots + 1]),
+    ]
+    for copy in copies:
+        copy.start()
     for n in range(slots):
         rows_buf[n] = state[n].astype(F32)
         total = jnp.zeros((blk, blk), F32)
@@ -453,7 +489,6 @@
         density_buf[n] = total / (phys * blk)
         copies.append(pltpu.make_async_copy(density_buf.at[n], density.at[n], sems.at[n]))
         copies[-1].start()
-    energy_out[0] = energy[0, 0]
     for copy in copies:
         copy.wait()
 
@@ -465,7 +500,6 @@
     side = chan * TILE
     vmem = pl.BlockSpec(memory_space=pltpu.VMEM)
     hbm = pl.BlockSpec(memory_space=pltpu.HBM)
-    smem = pl.BlockSpec(memory_space=pltpu.SMEM)
     dma = pltpu.SemaphoreType.DMA
     twice = lambda *spec: [pltpu.VMEM(*spec)] * 2
     outs = pl.pallas_call(
@@ -474,9 +508,13 @@
             jax.ShapeDtypeStruct((slots, wide, blk), BF16),
             jax.ShapeDtypeStruct((8, blk), F32),
         ),
-        in_specs=[hbm, hbm, hbm, vmem, vmem, vmem, vmem],
-        out_specs=(vmem, vmem),
+        in_specs=[hbm] * 7,
+        out_specs=(hbm, hbm),
         scratch_shapes=[
+            pltpu.VMEM((chan * phys * phys, chan), BF16),
+            pltpu.VMEM((1, 1), jnp.int32),
+            pltpu.VMEM((slots, wide, blk), BF16),
+            pltpu.VMEM((8, blk), F32),
             pltpu.VMEM((slots, wide, blk), BF16),
             pltpu.VMEM((slots, chan, blk, blk), BF16),
             pltpu.VMEM((slots, chan, blk, blk), BF16),
@@ -493,7 +531,7 @@
             pltpu.VMEM((regions, slots, blk), F32),
             pltpu.VMEM((8, blk), F32),
             pltpu.VMEM((sectors, 8, blk), F32),
-            dma((slots,)), dma((slots,)), dma((slots,)), dma((slots,)),
+            dma((slots,)), dma((slots,)), dma((slots,)), dma((slots,)), dma((4,)), dma((slots + 1,)),
             dma((2, regions)), dma((2, regions)),
             dma((sectors,)), dma((sectors,)),
         ],
@@ -513,11 +551,12 @@
             jax.ShapeDtypeStruct((1,), F32),
         ),
         in_specs=[vmem, vmem],
-        out_specs=(hbm, hbm, smem),
+        out_specs=(hbm, hbm, hbm),
         scratch_shapes=[
             pltpu.VMEM((slots, wide, blk), F32),
             pltpu.VMEM((slots, blk, blk), F32),
-            dma((slots + 1,)),
+            pltpu.SMEM((1,), F32),
+            dma((slots + 2,)),
         ],
     )(*outs)
     return (

time: 44.2 us -> 42.8 us (0.968)
  Pallas kernels: 42.7 us -> 41.4 us
    pallas_call x1, Pallas kernels: 40 us -> 39.1 us  [body(): pl.pallas_call(functools.partial(kernel, regions, sectors), out_shape=(ja...]
    pallas_call x1, Pallas kernels: 2.75 us -> 2.26 us  [body(): pl.pallas_call(finish, out_shape=(jax.ShapeDtypeStruct((slots, wide, blk)...]
where the time goes in v5:
time: 42.8 us; the launch traced here: 42.7 us
  Pallas kernels  41.4 us (97%)
  between operations  1.29 us (3%)
    pallas_call x1, Pallas kernels, body(): pl.pallas_call(functools.partial(kernel, regions, sectors), out_shape=(ja...  39.1 us
    pallas_call x1, Pallas kernels, body(): pl.pallas_call(finish, out_shape=(jax.ShapeDtypeStruct((slots, wide, blk)...  2.26 us

profile of v5, /device:TPU:2, one launch (start us, length us, event | category | flops | bytes accessed | tf_op | source)
XLA Modules:
  0.0 42.7 jit_solution(8239958395623462396)
XLA Ops:
  1.3 39.1 %shard_map.94 = (bf16[4,512,128]{2,1,0:T(8,128)(2,1)}, f32[8,128]{1,0:T(8,128)}) custom-call(bf16[4,512,128]{2,1,0:T(8,128)(2,1)} %bitcast.10, bf16[4,16,128,128]{3,2,1,0:T(8,128)(2,1)} %bitcast.8, bf16[4,16,128,128]{3,2,1,0:T(8,128)(2,1)} %bitcast.9, bf16[256,16]{1,0:T(8,128)(2,1)} %bitcast.11, f32[4,128]{1,0:T(4,128)} %bitcast.12, f32[4,128]{1,0:T(4,128)} %bitcast.13, ...), custom_call_target="tpu_custom_call" | custom-call | tf_op jit(solution)/shard_map/pallas_call | solution.py:505
  40.4 2.3 %shard_map.95 = (bf16[4,512,128]{2,1,0:T(8,128)(2,1)}, f32[4,128,128]{2,1,0:T(8,128)}, f32[1]{0:T(128)}) custom-call(bf16[4,512,128]{2,1,0:T(8,128)(2,1)} %get-tuple-element.8.state, f32[8,128]{1,0:T(8,128)} %get-tuple-element.9.energy), custom_call_target="tpu_custom_call" | custom-call | tf_op jit(solution)/shard_map/pallas_call | solution.py:546

commit v6 on v5

--- a/solution.py
+++ b/solution.py
@@ -51,13 +51,14 @@
     rounds = jnp.where(crossing, 0, slots // 2 * STEPS)
     singles = jnp.where(crossing, slots, 0)
     barrier = pltpu.get_barrier_semaphore()
+    far_first = sorted(range(1, sectors), key=lambda k: abs(2 * k - sectors))
+    for k in far_first:
+        pl.semaphore_signal(
+            barrier, 1, device_id={"sector": lax.rem(mine + k, sectors)}, device_id_type=MESH
+        )
     for k in range(1, regions):
         pl.semaphore_signal(
             barrier, 1, device_id={"region": lax.rem(me + k, regions)}, device_id_type=MESH
-        )
-    for k in range(1, sectors):
-        pl.semaphore_signal(
-            barrier, 1, device_id={"sector": lax.rem(mine + k, sectors)}, device_id_type=MESH
         )
     small = [
         pltpu.make_async_copy(src, dst, small_sem.at[i])
@@ -225,7 +226,8 @@
         return rights, [functools.partial(operator_part, q) for q in range(wide // (4 * TILE))]
 
     def close(n, j, vector, mixed, value, final=False):
-        held = {"along": [zero] * STEPS, "whole": zero, "norm": zero}
+        known = j + 1 if isinstance(j, int) else STEPS
+        held = {"along": [zero] * known, "whole": zero, "norm": zero}
 
         def left_part():
             rows = jnp.concatenate([left_in[n, u] for u in range(chan)], axis=1)
@@ -260,13 +262,13 @@
             held["norm"] = held["norm"] + sum8(probe * probe)
 
         def record_part():
-            numbers = [*held["shares"]]
+            numbers = list(enumerate(held["shares"]))
             if not final:
                 norm = spread_sum(held["norm"])
                 norms[n] = jnp.where(line8 == j + 1, norm, norms[n])
-                numbers += [held["length"], norm]
+                numbers += [(STEPS, held["length"]), (STEPS + 1, norm)]
             row = jnp.zeros((1, blk), F32)
-            for i, number in enumerate(numbers):
+            for i, number in numbers:
                 row = jnp.where(lane == 8 * j + i, number, row)
             part[...] = jnp.where((line8 == n) & (lane8 // 8 == j), row, part[...])
 
@@ -394,7 +396,7 @@
             device_id={"sector": lax.rem(mine + k, sectors)}, device_id_type=MESH,
         )
 
-    for k in sorted(range(1, sectors), key=lambda k: abs(2 * k - sectors)):
+    for k in far_first:
         copy_of(k, mine).start()
     for k in range(1, sectors):
         copy_of(k, lax.rem(mine + sectors - k, sectors)).wait()

time: 42.8 us -> 42.8 us (level)
  no operation moved by 1% of the time
where the time goes in v6:
time: 42.8 us; the launch traced here: 42.6 us
  Pallas kernels  41.3 us (96%)
  between operations  1.29 us (3%)
    pallas_call x1, Pallas kernels, body(): pl.pallas_call(functools.partial(kernel, regions, sectors), out_shape=(ja...  39.1 us
    pallas_call x1, Pallas kernels, body(): pl.pallas_call(finish, out_shape=(jax.ShapeDtypeStruct((slots, wide, blk)...  2.25 us

profile of v6, /device:TPU:2, one launch (start us, length us, event | category | flops | bytes accessed | tf_op | source)
XLA Modules:
  0.0 42.6 jit_solution(6187790556935291005)
XLA Ops:
  1.3 39.1 %shard_map.94 = (bf16[4,512,128]{2,1,0:T(8,128)(2,1)}, f32[8,128]{1,0:T(8,128)}) custom-call(bf16[4,512,128]{2,1,0:T(8,128)(2,1)} %bitcast.10, bf16[4,16,128,128]{3,2,1,0:T(8,128)(2,1)} %bitcast.8, bf16[4,16,128,128]{3,2,1,0:T(8,128)(2,1)} %bitcast.9, bf16[256,16]{1,0:T(8,128)(2,1)} %bitcast.11, f32[4,128]{1,0:T(4,128)} %bitcast.12, f32[4,128]{1,0:T(4,128)} %bitcast.13, ...), custom_call_target="tpu_custom_call" | custom-call | tf_op jit(solution)/shard_map/pallas_call | solution.py:507
  40.4 2.2 %shard_map.95 = (bf16[4,512,128]{2,1,0:T(8,128)(2,1)}, f32[4,128,128]{2,1,0:T(8,128)}, f32[1]{0:T(128)}) custom-call(bf16[4,512,128]{2,1,0:T(8,128)(2,1)} %get-tuple-element.8.state, f32[8,128]{1,0:T(8,128)} %get-tuple-element.9.energy), custom_call_target="tpu_custom_call" | custom-call | tf_op jit(solution)/shard_map/pallas_call | solution.py:548
